TPU v7x, 512 devices: a whole 4x4x16 slice. The times are simulated.
512 devices in a mesh: beh: 4 (over y), node: 128 (over x, z, core).
Axes of the slice: x: 4, y: 4, z: 16, core: 2. Of those that a mesh axis runs over, the one named last changes fastest.
Arguments:
- embeddings: bfloat16 [262144, 128], P('node'), may hold values from -16 to 16, as said below
- adjacency: bfloat16 [4, 14336, 128, 128], P('beh', 'node'), may hold values from -0.1875 to 0.1875
- tile_rows: int32 [4, 14336], P('beh', 'node'), may hold values from 0 to 15
- tile_cols: int32 [4, 14336], P('beh', 'node'), may hold values from 0 to 63
- tile_count: int32 [4, 128], P('beh', 'node'), may hold values from 28 to 112, as said below
- need_ids: int32 [4, 8192], P('beh', 'node'), may hold values from 0 to 2047, as said below
- w_query: bfloat16 [128, 128], replicated, may hold values from -0.5 to 0.5
- w_key: bfloat16 [128, 128], replicated, may hold values from -0.5 to 0.5
- w_value: bfloat16 [128, 128], replicated, may hold values from -0.5 to 0.5
- w_out: bfloat16 [128, 128], replicated, may hold values from -0.5 to 0.5
- mlp_gain: float32 [128], replicated, may hold values from 0.1 to 1.9
- w_up: bfloat16 [128, 512], replicated, may hold values from -0.5 to 0.5
- w_down: bfloat16 [512, 128], replicated, may hold values from -0.25 to 0.25
Outputs:
- merged: bfloat16 [4, 262144, 128], P('beh', 'node')
Inputs may be any that keep to these rules, and one draw needn't show every extreme that they name: `tile_count`: live slots of one behavior and shard; every behavior has a shard with all 112 slots live. `need_ids`: for each behavior b and shard n, entry n * 64 + m (m < 64) names a block owned by shard 2 m or shard 2 m + 1, block g being owned by shard g // 16. `embeddings`: entries keep within the stated bound.
All inputs are finite; a program needn't handle non-finite values.
Results may differ from a plain program's by a relative error of at most 0.0077.
Values may be sent and summed in bfloat16 or wider, within the bound.
A program may use at most 64 MiB of HBM per device.

v0:
```python
import math

import jax
import jax.numpy as jnp
from jax import lax
from jax.sharding import PartitionSpec as P

TB = 128
HEADS = 4
HEAD = 32


def partner(value, axis, stride):
    mask = 2**stride
    pairs = [(source, source ^ mask) for source in range(lax.axis_size(axis))]
    return lax.ppermute(value, axis, pairs)


def laid_out(tiles, dim):
    lengths = list(tiles.shape[1:])
    lengths[dim] *= tiles.shape[0]
    return jnp.moveaxis(tiles, 0, dim).reshape(lengths)


def copy_for_each(value, axis):
    devices = lax.axis_size(axis)
    return lax.all_to_all(
        jnp.broadcast_to(value[None], (devices, *value.shape)), axis, 0, 0, tiled=True
    )


def collect(value, axis, dim):
    return laid_out(copy_for_each(value, axis), dim)


def merge_behaviors(behaviors, queries, w_query, w_key, w_value, w_out, mlp_gain, w_up, w_down):
    count_k, row_count, feature = behaviors.shape
    count_q = queries.shape[0]
    flat_keys = behaviors.reshape(count_k * row_count, feature)
    key_rows = jnp.dot(flat_keys, w_key, preferred_element_type=jnp.float32).reshape(
        count_k, row_count, HEADS, HEAD
    )
    value_rows = jnp.dot(flat_keys, w_value, preferred_element_type=jnp.float32).reshape(
        count_k, row_count, HEADS, HEAD
    )
    flat_queries = queries.reshape(count_q * row_count, feature)
    query_rows = jnp.dot(flat_queries, w_query, preferred_element_type=jnp.float32).reshape(
        count_q, row_count, HEADS, HEAD
    )
    scores = jnp.einsum(
        "qrhe,krhe->qrhk", query_rows, key_rows, precision=lax.Precision.HIGHEST
    ) / math.sqrt(HEAD)
    highest = jnp.max(scores, axis=-1, keepdims=True)
    weights = jnp.exp(scores - highest)
    weights = weights / jnp.sum(weights, axis=-1, keepdims=True)
    mixture = jnp.einsum("qrhk,krhe->qrhe", weights, value_rows, precision=lax.Precision.HIGHEST)
    mixture = mixture.reshape(count_q * row_count, feature).astype(jnp.bfloat16)
    residual = flat_queries.astype(jnp.float32) + jnp.dot(
        mixture, w_out, preferred_element_type=jnp.float32
    )
    meansq = jnp.mean(residual * residual, axis=-1, keepdims=True)
    normed = (residual * lax.rsqrt(meansq + 1e-06) * mlp_gain).astype(jnp.bfloat16)
    hidden = jax.nn.silu(jnp.dot(normed, w_up, preferred_element_type=jnp.float32)).astype(
        jnp.bfloat16
    )
    result = residual + jnp.dot(hidden, w_down, preferred_element_type=jnp.float32)
    return result.astype(jnp.bfloat16).reshape(count_q, row_count, feature)


def shards(
    embeddings,
    adjacency,
    tile_rows,
    tile_cols,
    tile_count,
    need_ids,
    w_query,
    w_key,
    w_value,
    w_out,
    mlp_gain,
    w_up,
    w_down,
):
    peer_count = lax.axis_size("node")
    node_rows, feature = embeddings.shape
    block_count = node_rows // TB
    needed = need_ids[0]
    owners = needed // block_count
    within = needed % block_count
    matches = owners[:, None] == jnp.arange(peer_count, dtype=jnp.int32)[None, :]
    request = jnp.sum(jnp.where(matches, within[:, None] + 1, 0), axis=0)
    peer_ids = jnp.arange(peer_count, dtype=jnp.int32)
    partner_ids = peer_ids + 1 - 2 * (peer_ids % 2)
    request_pair = jnp.stack([request, request[partner_ids]], axis=1)
    incoming = lax.all_to_all(request_pair, "node", split_axis=0, concat_axis=0, tiled=True)
    own_blocks = embeddings.reshape(block_count, TB, feature)
    parity = lax.axis_index("node") % 2
    partner_rows = partner(embeddings, "node", 0)
    other_blocks = partner_rows.reshape(block_count, TB, feature)
    own_code = jnp.where(incoming[:, 0] > 0, parity * block_count + incoming[:, 0], 0)
    other_code = jnp.where(incoming[:, 1] > 0, (1 - parity) * block_count + incoming[:, 1], 0)
    codes = own_code + other_code
    pair_stack = jnp.where(
        parity == 0,
        jnp.concatenate([own_blocks, other_blocks], axis=0),
        jnp.concatenate([other_blocks, own_blocks], axis=0),
    )
    half_rows = TB // 2
    halves = lax.dynamic_slice_in_dim(pair_stack, parity * half_rows, half_rows, 1)
    chooser = (codes[:, None] - 1 == jnp.arange(2 * block_count, dtype=jnp.int32)[None, :]).astype(
        jnp.bfloat16
    )
    outgoing = jnp.einsum(
        "pk,kid->pid", chooser, halves, preferred_element_type=jnp.float32
    ).astype(jnp.bfloat16)
    arrived = lax.all_to_all(outgoing, "node", split_axis=0, concat_axis=0, tiled=True)
    pairs = arrived.reshape(peer_count // 2, TB, feature)
    sources = pairs[owners[tile_cols[0]] // 2]
    product = jnp.einsum("tij,tjd->tid", adjacency[0], sources, preferred_element_type=jnp.float32)
    active = jnp.arange(adjacency.shape[1], dtype=jnp.int32) < tile_count[0, 0]
    select = (
        (tile_rows[0][:, None] == jnp.arange(block_count, dtype=jnp.int32)[None, :])
        & active[:, None]
    ).astype(jnp.float32)
    summed = jnp.einsum("tb,tid->bid", select, product, precision=lax.Precision.HIGHEST).reshape(
        node_rows, feature
    )
    spread = (summed + embeddings.astype(jnp.float32)).astype(jnp.bfloat16)
    everyone = collect(spread[None], "beh", 0)
    index_now = lax.axis_index("beh")
    mine = lax.dynamic_slice_in_dim(everyone, index_now, 1, 0)
    return merge_behaviors(everyone, mine, w_query, w_key, w_value, w_out, mlp_gain, w_up, w_down)


def solution(mesh):
    in_specs = (
        P("node", None),
        P("beh", "node", None, None),
        P("beh", "node"),
        P("beh", "node"),
        P("beh", "node"),
        P("beh", "node"),
        P(),
        P(),
        P(),
        P(),
        P(),
        P(),
        P(),
    )
    out_specs = P("beh", "node", None)
    return jax.shard_map(shards, mesh=mesh, in_specs=in_specs, out_specs=out_specs, check_vma=False)
```

profile of v0, /device:TPU:1, one launch (start us, length us, event | category | flops | bytes accessed | tf_op | source)
XLA Modules:
  0.0 212.6 jit_solution(727437379977541010)
XLA Ops:
  0.0 8.9 %collective-permute-start = (bf16[2048,128]{1,0:T(8,128)(2,1)}, bf16[2048,128]{1,0:T(8,128)(2,1)S(1)}, u32[]{:S(2)}, u32[]{:S(2)}) collective-permute-start(bf16[2048,128]{1,0:T(8,128)(2,1)} %param.13), channel_id=1, source_target_pairs={{0,1},{1,0},{2,3},{3,2},{4,5},{5,4},{6,7},{7,6},{8,9},{9,8},{10,11... | collective-permute-start | bytes 1572872 | tf_op jit(solution)/shard_map/ppermute | solution.py:16
  8.9 0.1 fusion.32
  9.0 0.7 and_select_fusion.2
  9.8 1.2 gather_fusion
  11.0 0.7 copy.68
  11.8 13.7 %all-to-all-start = ((s32[128,1,2]{2,1,0:T(1,128)}), s32[128,1,2]{2,1,0:T(1,128)S(1)}, u32[]{:S(2)}, u32[]{:S(2)}) async-start(s32[128,1,2]{2,1,0:T(1,128)} %copy.68), calls=%async_computation | async-start | bytes 131072 | tf_op jit(solution)/shard_map/all_to_all | solution.py:96
  25.5 1.4 copy.69
  26.9 13.6 %all-to-all-done = s32[128,1,2]{2,1,0:T(1,128)S(1)} async-done(((s32[128,1,2]{2,1,0:T(1,128)}), s32[128,1,2]{2,1,0:T(1,128)S(1)}, u32[]{:S(2)}, u32[]{:S(2)}) %all-to-all-start) | async-done | bytes 1056 | tf_op jit(solution)/shard_map/all_to_all | solution.py:96
  40.4 0.2 add_reduce_fusion
  40.6 0.3 copy.70
  41.0 0.8 convolution_convert_fusion
  41.7 2.7 %copy.73 = bf16[128,64,128]{2,1,0:T(8,128)(2,1)} copy(bf16[128,64,128]{2,0,1:T(8,128)(2,1)S(1)} %convolution_convert_fusion) | data formatting | bytes 4194304 | tf_op jit(solution)/shard_map/convert_element_type | solution.py:116
  44.4 6.6 %all-to-all-start.1 = ((bf16[128,64,128]{2,1,0:T(8,128)(2,1)}), bf16[128,64,128]{2,1,0:T(8,128)(2,1)S(1)}, u32[]{:S(2)}, u32[]{:S(2)}) async-start(bf16[128,64,128]{2,1,0:T(8,128)(2,1)} %copy.73), calls=%async_computation.1 | async-start | bytes 4194304 | tf_op jit(solution)/shard_map/all_to_all | solution.py:117
  51.1 1.2 gather_fusion.1
  53.0 97.3 %all-to-all-done.1 = bf16[128,64,128]{2,1,0:T(8,128)(2,1)S(1)} async-done(((bf16[128,64,128]{2,1,0:T(8,128)(2,1)}), bf16[128,64,128]{2,1,0:T(8,128)(2,1)S(1)}, u32[]{:S(2)}, u32[]{:S(2)}) %all-to-all-start.1) | async-done | bytes 2097184 | tf_op jit(solution)/shard_map/all_to_all | solution.py:117
  150.3 3.0 %gather_fusion.2 = bf16[112,128,128]{2,1,0:T(8,128)(2,1)} fusion(bf16[64,128,128]{2,1,0:T(8,128)(2,1)S(1)} %bitcast.103, s32[1024]{0:T(1024)S(1)} %pad_clamp_fusion), kind=kCustom, calls=%fused_computation.2 | custom fusion | bytes 7340480 | tf_op jit(solution)/shard_map/gather | solution.py:119
  153.3 8.8 %fusion.3 = f32[112,128,128]{1,2,0:T(8,128)} fusion(bf16[112,128,128]{2,1,0:T(8,128)(2,1)} %gather_fusion.2, bf16[1,112,128,128]{3,2,1,0:T(8,128)(2,1)} %param.14), kind=kOutput, calls=%fused_computation.9 | convolution fusion | flops 469762048 | bytes 14680064 | tf_op jit(solution)/shard_map/tij,tjd->tid/dot_general | solution.py:120
  162.1 8.5 %copy.75 = f32[112,128,128]{2,0,1:T(8,128)} copy(f32[112,128,128]{1,2,0:T(8,128)} %fusion.3) | data formatting | bytes 14680064 | tf_op jit(solution)/shard_map/tij,tjd->tid/dot_general | solution.py:120
  170.6 4.7 %fusion.39 = f32[16,128,128]{2,0,1:T(8,128)S(1)} fusion(f32[112,128,128]{2,0,1:T(8,128)} %copy.75, s32[112]{0:T(128)S(1)} %bitcast.112, pred[112]{0:T(512)(128)(4,1)S(1)} %iota_compare_fusion.3), kind=kOutput, calls=%fused_computation.60 | convolution fusion | flops 352325120 | bytes 8389168 | tf_op jit(solution)/shard_map/tb,tid->bid/dot_general | solution.py:126
  175.3 0.3 copy.76
  175.7 0.1 fusion.12
  175.8 1.6 broadcast_in_dim.19
  177.4 4.2 %all-to-all-start.2 = ((bf16[4,1,2048,128]{3,2,1,0:T(8,128)(2,1)}), bf16[4,1,2048,128]{3,2,1,0:T(8,128)(2,1)S(1)}, u32[]{:S(2)}, u32[]{:S(2)}) async-start(bf16[4,1,2048,128]{3,2,1,0:T(8,128)(2,1)} %broadcast_in_dim.19), calls=%async_computation.2 | async-start | bytes 4194304 | tf_op jit(solution)/shard_map/all_to_all | solution.py:27
  181.7 0.1 copy.78
  181.9 0.1 copy.77
  182.0 25.2 %all-to-all-done.2 = bf16[4,1,2048,128]{3,2,1,0:T(8,128)(2,1)S(1)} async-done(((bf16[4,1,2048,128]{3,2,1,0:T(8,128)(2,1)}), bf16[4,1,2048,128]{3,2,1,0:T(8,128)(2,1)S(1)}, u32[]{:S(2)}, u32[]{:S(2)}) %all-to-all-start.2) | async-done | bytes 2097184 | tf_op jit(solution)/shard_map/all_to_all | solution.py:27
  207.2 0.3 fusion.18
  207.5 0.8 multiply_reduce_fusion.1
  208.3 0.2 fusion.51
  208.7 0.7 multiply_reduce_fusion
  209.4 0.6 multiply_reduce_fusion.2
  210.1 2.6 %fusion.7 = bf16[1,2048,128]{2,1,0:T(8,128)(2,1)} fusion(f32[2048,128]{1,0:T(8,128)S(1)} %get-tuple-element.10, bf16[512,128]{1,0:T(8,128)(2,1)S(1)} %copy-done, bf16[128,512]{1,0:T(8,128)(2,1)S(1)} %copy-done.7, f32[128]{0:T(128)S(1)} %copy-done.9, f32[2048]{0:T(1024)S(1)} %add_rsqrt_fusion), kind=kOutput, calls=%fused_computation.13 | convolution fusion | flops 543424512 | bytes 1843712 | tf_op jit(solution)/shard_map/dot_general | solution.py:66
  (33 shorter events, 0.5 us)
Async XLA Ops:
  0.0 210.0 %copy-start = (bf16[512,128]{1,0:T(8,128)(2,1)S(1)}, bf16[512,128]{1,0:T(8,128)(2,1)}, u32[]{:S(2)}) copy-start(bf16[512,128]{1,0:T(8,128)(2,1)} %param.25) | copy-start | bytes 393220
  0.0 40.6 %collective-permute-start = (bf16[2048,128]{1,0:T(8,128)(2,1)}, bf16[2048,128]{1,0:T(8,128)(2,1)S(1)}, u32[]{:S(2)}, u32[]{:S(2)}) collective-permute-start(bf16[2048,128]{1,0:T(8,128)(2,1)} %param.13), channel_id=1, source_target_pairs={{0,1},{1,0},{2,3},{3,2},{4,5},{5,4},{6,7},{7,6},{8,9},{9,8},{10,11... | collective-permute-start | bytes 1572872 | tf_op jit(solution)/shard_map/ppermute | solution.py:16
  11.8 28.6 %all-to-all-start = ((s32[128,1,2]{2,1,0:T(1,128)}), s32[128,1,2]{2,1,0:T(1,128)S(1)}, u32[]{:S(2)}, u32[]{:S(2)}) async-start(s32[128,1,2]{2,1,0:T(1,128)} %copy.68), calls=%async_computation | async-start | bytes 131072 | tf_op jit(solution)/shard_map/all_to_all | solution.py:96
  41.7 9.3 %copy-start.8 = (s32[1,112]{1,0:T(1,128)S(1)}, s32[1,112]{1,0:T(1,128)}, u32[]{:S(2)}) copy-start(s32[1,112]{1,0:T(1,128)} %param.16) | copy-start | bytes 1348
  44.4 105.9 %all-to-all-start.1 = ((bf16[128,64,128]{2,1,0:T(8,128)(2,1)}), bf16[128,64,128]{2,1,0:T(8,128)(2,1)S(1)}, u32[]{:S(2)}, u32[]{:S(2)}) async-start(bf16[128,64,128]{2,1,0:T(8,128)(2,1)} %copy.73), calls=%async_computation.1 | async-start | bytes 4194304 | tf_op jit(solution)/shard_map/all_to_all | solution.py:117
  162.1 8.5 %copy-start.6 = (s32[1,112]{1,0:T(1,128)S(1)}, s32[1,112]{1,0:T(1,128)}, u32[]{:S(2)}) copy-start(s32[1,112]{1,0:T(1,128)} %param.15) | copy-start | bytes 1348
  170.6 5.0 %copy-start.1 = (bf16[2048,128]{1,0:T(8,128)(2,1)S(1)}, bf16[2048,128]{1,0:T(8,128)(2,1)}, u32[]{:S(2)}) copy-start(bf16[2048,128]{1,0:T(8,128)(2,1)} %param.13) | copy-start | bytes 1572868
  175.8 5.8 %copy-start.3 = (bf16[128,128]{1,0:T(8,128)(2,1)S(1)}, bf16[128,128]{1,0:T(8,128)(2,1)}, u32[]{:S(2)}) copy-start(bf16[128,128]{1,0:T(8,128)(2,1)} %param.19) | copy-start | bytes 98308
  175.8 6.0 %copy-start.4 = (bf16[128,128]{1,0:T(8,128)(2,1)S(1)}, bf16[128,128]{1,0:T(8,128)(2,1)}, u32[]{:S(2)}) copy-start(bf16[128,128]{1,0:T(8,128)(2,1)} %param.20) | copy-start | bytes 98308
  175.8 6.1 %copy-start.5 = (bf16[128,128]{1,0:T(8,128)(2,1)S(1)}, bf16[128,128]{1,0:T(8,128)(2,1)}, u32[]{:S(2)}) copy-start(bf16[128,128]{1,0:T(8,128)(2,1)} %param.21) | copy-start | bytes 98308
  177.4 29.7 %all-to-all-start.2 = ((bf16[4,1,2048,128]{3,2,1,0:T(8,128)(2,1)}), bf16[4,1,2048,128]{3,2,1,0:T(8,128)(2,1)S(1)}, u32[]{:S(2)}, u32[]{:S(2)}) async-start(bf16[4,1,2048,128]{3,2,1,0:T(8,128)(2,1)} %broadcast_in_dim.19), calls=%async_computation.2 | async-start | bytes 4194304 | tf_op jit(solution)/shard_map/all_to_all | solution.py:27
  208.3 1.1 copy-start.2
  208.7 1.4 copy-start.7
  208.7 1.4 copy-start.9
where the time goes:
time: 214 us; the launch traced here: 213 us
  waiting for transfers between devices  136 us (64%)
  starting transfers between devices  33.3 us (16%)
  local copies, waits for them, and re-layouts  21.5 us (10%)
  matrix products  19.2 us (9%)
    all_to_all x1, waiting for transfers between devices, shards(): lax.all_to_all(outgoing, 'node', split_axis=0, concat_axis=0, tiled=True)  97.3 us
    all_to_all x1, waiting for transfers between devices, copy_for_each(): lax.all_to_all(jnp.broadcast_to(value[None], (devices, *value.shape)), ax...  25.2 us
    all_to_all x1, starting transfers between devices, shards(): lax.all_to_all(request_pair, 'node', split_axis=0, concat_axis=0, tiled=T...  13.7 us
    all_to_all x1, waiting for transfers between devices, shards(): lax.all_to_all(request_pair, 'node', split_axis=0, concat_axis=0, tiled=T...  13.6 us
    ppermute x1, starting transfers between devices, partner(): return lax.ppermute(value, axis, pairs)  8.87 us
    dot_general x1, matrix products, shards(): jnp.einsum('tij,tjd->tid', adjacency[0], sources, preferred_element_type=...  8.83 us
    dot_general x1, local copies, waits for them, and re-layouts, shards(): jnp.einsum('tij,tjd->tid', adjacency[0], sources, preferred_element_type=...  8.47 us
    all_to_all x1, starting transfers between devices, shards(): lax.all_to_all(outgoing, 'node', split_axis=0, concat_axis=0, tiled=True)  6.61 us
  transfers between devices with their start and end apart: 4, of which 3 were waited for; matrix products, arithmetic and copies ran while one was open for 3% of the time, Pallas kernels for 0%

commit v1 on v0

v1 whole, which is shorter than its diff:
```python
import functools
import math

import jax
import jax.numpy as jnp
from jax import lax
from jax.experimental import pallas as pl
from jax.experimental.pallas import tpu as pltpu
from jax.sharding import PartitionSpec as P

TB = 128
HEADS = 4
HEAD = 32
MESH = pl.DeviceIdType.MESH
STEPS = 8


def place():
    y = lax.axis_index("beh")
    n = lax.axis_index("node")
    return n // 32, y, lax.rem(n // 2, 16), lax.rem(n, 2)


def device(x, y, z, k):
    return (y, (x * 16 + z) * 2 + k)


def gather_kernel(emb_ref, need_ref, out_ref, *scratch):
    chunks = scratch[:9]
    picked, need_v, need_s = scratch[9:12]
    own_sem, pair_send, pair_recv, ring_send, ring_recv = scratch[12:17]
    ask_send, ask_recv, smem_sem, xy_send, xy_recv = scratch[17:]
    x, y, z, k = place()
    me = x * 8 + y * 2 + k
    part = y * 2 + k
    above = device(x, y, lax.rem(z + 1, 16), k)
    below = device(x, y, lax.rem(z + 15, 16), k)
    twin = device(x, y, z, 1 - k)

    def reader(r):
        return device(r // 8, lax.rem(r, 8) // 2, z, lax.rem(r, 2))

    own = pltpu.make_async_copy(
        emb_ref.at[:, part], chunks[0].at[pl.ds(k * 16, 16)], own_sem
    )
    own.start()

    barrier = pltpu.get_barrier_semaphore()

    @pl.loop(1, 32)
    def _(i):
        pl.semaphore_signal(
            barrier, inc=1, device_id=reader(lax.rem(me + i, 32)), device_id_type=MESH
        )

    for neighbour in (above, below):
        pl.semaphore_signal(barrier, inc=1, device_id=neighbour, device_id_type=MESH)
    pl.semaphore_wait(barrier, 33)

    pair = pltpu.make_async_remote_copy(
        src_ref=emb_ref.at[:, y * 2 + 1 - k],
        dst_ref=chunks[0].at[pl.ds(k * 16, 16)],
        send_sem=pair_send,
        recv_sem=pair_recv,
        device_id=twin,
        device_id_type=MESH,
    )
    pair.start()

    @pl.loop(1, 32)
    def _(i):
        pltpu.make_async_remote_copy(
            src_ref=need_ref,
            dst_ref=need_v.at[me],
            send_sem=ask_send,
            recv_sem=ask_recv,
            device_id=reader(lax.rem(me + i, 32)),
            device_id_type=MESH,
        ).start()

    pltpu.make_async_copy(need_ref, need_v.at[me], ask_recv).start()

    def half(step, way, h):
        if step == 0 or step == STEPS:
            return chunks[step].at[pl.ds(h * 16, 16)]
        return chunks[step].at[way, pl.ds(h * 16, 16)]

    def hop(step, way, h):
        return pltpu.make_async_remote_copy(
            src_ref=half(step, way, h),
            dst_ref=half(step + 1, way, h),
            send_sem=ring_send.at[way, step, h],
            recv_sem=ring_recv.at[way, step, h],
            device_id=above if way == 0 else below,
            device_id_type=MESH,
        )

    hops = {}

    def forward(step):
        for h in range(2):
            for way in range(2):
                if step > 0:
                    hops[(step - 1, way, h)].wait_recv()
                if step < STEPS - 1 or way == h:
                    hops[(step, way, h)] = hop(step, way, h)
                    hops[(step, way, h)].start()

    def pick(step):
        @pl.loop(0, 32)
        def _(r):
            if step == 0:
                index = lax.rem(need_s[r, 0, x * 16 + z], 32)
                picked[r, 0] = chunks[0][index]
            elif step == STEPS:
                index = lax.rem(need_s[r, 0, x * 16 + lax.rem(z + 8, 16)], 32)
                picked[r, 15] = chunks[STEPS][index]
            else:
                index = lax.rem(need_s[r, 0, x * 16 + lax.rem(z + 16 - step, 16)], 32)
                picked[r, 2 * step - 1] = chunks[step][0, index]
                index = lax.rem(need_s[r, 0, x * 16 + lax.rem(z + step, 16)], 32)
                picked[r, 2 * step] = chunks[step][1, index]

    def deliver(step):
        if step == 0:
            slots = pl.ds(0, 1)
        elif step == STEPS:
            slots = pl.ds(15, 1)
        else:
            slots = pl.ds(2 * step - 1, 2)

        @pl.loop(1, 32)
        def _(i):
            r = lax.rem(me + i, 32)
            pltpu.make_async_remote_copy(
                src_ref=picked.at[r, slots],
                dst_ref=out_ref.at[x, slots, part],
                send_sem=xy_send,
                recv_sem=xy_recv,
                device_id=reader(r),
                device_id_type=MESH,
            ).start()

        pltpu.make_async_copy(
            picked.at[me, slots], out_ref.at[x, slots, part], xy_recv
        ).start()

    own.wait()
    pair.wait_recv()
    forward(0)
    pltpu.make_async_copy(need_v, need_v, ask_recv).wait()
    table = pltpu.make_async_copy(need_v, need_s, smem_sem)
    table.start()
    table.wait()
    pick(0)
    deliver(0)
    for step in range(1, STEPS):
        forward(step)
        pick(step)
        deliver(step)
    hops[(STEPS - 1, 0, 0)].wait_recv()
    hops[(STEPS - 1, 1, 1)].wait_recv()
    pick(STEPS)
    deliver(STEPS)

    pair.wait_send()
    for one in hops.values():
        one.wait_send()
    asked = need_v.at[pl.ds(0, 31)]
    pltpu.make_async_copy(asked, asked, ask_send).wait()
    sent = picked.at[pl.ds(0, 31)]
    pltpu.make_async_copy(sent, sent, xy_send).wait()
    pltpu.make_async_copy(out_ref, out_ref, xy_recv).wait()


def gather_sources(embeddings, need):
    dma = pltpu.SemaphoreType.DMA
    one = pltpu.VMEM((32, 16, 128), jnp.bfloat16)
    two = pltpu.VMEM((2, 32, 16, 128), jnp.bfloat16)
    return pl.pallas_call(
        gather_kernel,
        out_shape=jax.ShapeDtypeStruct((4, 16, 8, 16, 128), jnp.bfloat16),
        in_specs=[pl.BlockSpec(memory_space=pl.ANY), pl.BlockSpec(memory_space=pl.ANY)],
        out_specs=pl.BlockSpec(memory_space=pltpu.VMEM),
        scratch_shapes=[
            one,
            *([two] * 7),
            one,
            pltpu.VMEM((32, 16, 16, 128), jnp.bfloat16),
            pltpu.VMEM((32, 1, 64), jnp.int32),
            pltpu.SMEM((32, 1, 64), jnp.int32),
            dma,
            dma,
            dma,
            dma((2, 8, 2)),
            dma((2, 8, 2)),
            dma,
            dma,
            dma,
            dma,
            dma,
        ],
        compiler_params=pltpu.CompilerParams(
            collective_id=0, has_side_effects=True, vmem_limit_bytes=16 * 2**20
        ),
        name="gather_sources",
    )(embeddings.reshape(16, 8, 16, 128), need)


GROUP = 16
TILES = 112


def spread_kernel(rows_ref, cols_ref, count_ref, src_ref, emb_ref, adj_ref, out_ref, tiles, acc, sems):
    z = place()[2]
    count = count_ref[0, 0]

    def load(g):
        span = pl.ds(g * GROUP, GROUP)
        return pltpu.make_async_copy(adj_ref.at[span], tiles.at[span], sems.at[g])

    for g in range(TILES // GROUP):
        load(g).start()
    acc[0:16] = emb_ref[...].astype(jnp.float32)

    def add(t):
        col = cols_ref[0, t]
        away = lax.rem(lax.rem(col, 16) - z + 16, 16)
        slot = jnp.where(away < 8, 2 * away, jnp.where(away == 8, 15, 31 - 2 * away))
        row = jnp.where(t < count, rows_ref[0, t], 16)
        product = jnp.dot(
            tiles[t], src_ref[(col // 16) * 16 + slot], preferred_element_type=jnp.float32
        )
        acc[row] += product

    for g in range(TILES // GROUP):
        load(g).wait()

        @pl.loop(0, GROUP // 4)
        def _(i):
            @pl.when(g * GROUP + i * 4 < count)
            def _():
                for j in range(4):
                    add(g * GROUP + i * 4 + j)

    out_ref[...] = acc[0:16].astype(jnp.bfloat16)


def spread_rows(rows, cols, count, sources, embeddings, adjacency):
    smem = pl.BlockSpec(memory_space=pltpu.SMEM)
    vmem = pl.BlockSpec(memory_space=pltpu.VMEM)
    return pl.pallas_call(
        spread_kernel,
        out_shape=jax.ShapeDtypeStruct((16, 128, 128), jnp.bfloat16),
        in_specs=[smem, smem, smem, vmem, vmem, pl.BlockSpec(memory_space=pl.ANY)],
        out_specs=vmem,
        scratch_shapes=[
            pltpu.VMEM((TILES, 128, 128), jnp.bfloat16),
            pltpu.VMEM((17, 128, 128), jnp.float32),
            pltpu.SemaphoreType.DMA((TILES // GROUP,)),
        ],
        compiler_params=pltpu.CompilerParams(vmem_limit_bytes=20 * 2**20),
        name="spread_rows",
    )(rows, cols, count, sources.reshape(64, 128, 128), embeddings.reshape(16, 128, 128), adjacency)


def laid_out(tiles, dim):
    lengths = list(tiles.shape[1:])
    lengths[dim] *= tiles.shape[0]
    return jnp.moveaxis(tiles, 0, dim).reshape(lengths)


def copy_for_each(value, axis):
    devices = lax.axis_size(axis)
    return lax.all_to_all(
        jnp.broadcast_to(value[None], (devices, *value.shape)), axis, 0, 0, tiled=True
    )


def collect(value, axis, dim):
    return laid_out(copy_for_each(value, axis), dim)


def merge_behaviors(behaviors, queries, w_query, w_key, w_value, w_out, mlp_gain, w_up, w_down):
    count_k, row_count, feature = behaviors.shape
    count_q = queries.shape[0]
    flat_keys = behaviors.reshape(count_k * row_count, feature)
    key_rows = jnp.dot(flat_keys, w_key, preferred_element_type=jnp.float32).reshape(
        count_k, row_count, HEADS, HEAD
    )
    value_rows = jnp.dot(flat_keys, w_value, preferred_element_type=jnp.float32).reshape(
        count_k, row_count, HEADS, HEAD
    )
    flat_queries = queries.reshape(count_q * row_count, feature)
    query_rows = jnp.dot(flat_queries, w_query, preferred_element_type=jnp.float32).reshape(
        count_q, row_count, HEADS, HEAD
    )
    scores = jnp.einsum(
        "qrhe,krhe->qrhk", query_rows, key_rows, precision=lax.Precision.HIGHEST
    ) / math.sqrt(HEAD)
    highest = jnp.max(scores, axis=-1, keepdims=True)
    weights = jnp.exp(scores - highest)
    weights = weights / jnp.sum(weights, axis=-1, keepdims=True)
    mixture = jnp.einsum("qrhk,krhe->qrhe", weights, value_rows, precision=lax.Precision.HIGHEST)
    mixture = mixture.reshape(count_q * row_count, feature).astype(jnp.bfloat16)
    residual = flat_queries.astype(jnp.float32) + jnp.dot(
        mixture, w_out, preferred_element_type=jnp.float32
    )
    meansq = jnp.mean(residual * residual, axis=-1, keepdims=True)
    normed = (residual * lax.rsqrt(meansq + 1e-06) * mlp_gain).astype(jnp.bfloat16)
    hidden = jax.nn.silu(jnp.dot(normed, w_up, preferred_element_type=jnp.float32)).astype(
        jnp.bfloat16
    )
    result = residual + jnp.dot(hidden, w_down, preferred_element_type=jnp.float32)
    return result.astype(jnp.bfloat16).reshape(count_q, row_count, feature)


def shards(
    embeddings,
    adjacency,
    tile_rows,
    tile_cols,
    tile_count,
    need_ids,
    w_query,
    w_key,
    w_value,
    w_out,
    mlp_gain,
    w_up,
    w_down,
):
    sources = gather_sources(embeddings, need_ids)
    spread = spread_rows(tile_rows, tile_cols, tile_count, sources, embeddings, adjacency[0])
    spread = spread.reshape(embeddings.shape)
    everyone = collect(spread[None], "beh", 0)
    index_now = lax.axis_index("beh")
    mine = lax.dynamic_slice_in_dim(everyone, index_now, 1, 0)
    return merge_behaviors(everyone, mine, w_query, w_key, w_value, w_out, mlp_gain, w_up, w_down)


def solution(mesh):
    in_specs = (
        P("node", None),
        P("beh", "node", None, None),
        P("beh", "node"),
        P("beh", "node"),
        P("beh", "node"),
        P("beh", "node"),
        P(),
        P(),
        P(),
        P(),
        P(),
        P(),
        P(),
    )
    out_specs = P("beh", "node", None)
    return jax.shard_map(shards, mesh=mesh, in_specs=in_specs, out_specs=out_specs, check_vma=False)
```

time: 214 us -> 106 us (0.50)
  waiting for transfers between devices: 136 us -> 25.2 us
  Pallas kernels: 0 us -> 61.7 us
  starting transfers between devices: 33.3 us -> 3.61 us
  matrix products: 19.2 us -> 4.96 us
  local copies, waits for them, and re-layouts: 21.5 us -> 8.15 us
    all_to_all x2 -> x0, waiting for transfers between devices: 111 us -> none  [the longest x1 97.3 us: shards(): lax.all_to_all(outgoing, 'node', split_axis=0, concat_axis=0, tiled=True)]
    pallas_call x0 -> x2, Pallas kernels: none -> 61.7 us  [the longest x1 56 us: gather_sources(): pl.pallas_call(gather_kernel, out_shape=jax.ShapeDtypeStruct((4, 16, 8, 1...]
    all_to_all x2 -> x0, starting transfers between devices: 20.3 us -> none  [the longest x1 13.7 us: shards(): lax.all_to_all(request_pair, 'node', split_axis=0, concat_axis=0, tiled=T...]
    dot_general x3 -> x0, matrix products: 14.3 us -> none  [the longest x1 8.83 us: shards(): jnp.einsum('tij,tjd->tid', adjacency[0], sources, preferred_element_type=...]
    ppermute x1 -> x0, starting transfers between devices: 8.87 us -> none  [partner(): return lax.ppermute(value, axis, pairs)]
    dot_general x2 -> x0, local copies, waits for them, and re-layouts: 8.81 us -> none  [the longest x1 8.47 us: shards(): jnp.einsum('tij,tjd->tid', adjacency[0], sources, preferred_element_type=...]
    unnamed x24 -> x30, local copies, waits for them, and re-layouts: 0.48 us -> 6.54 us
    gather x3 -> x0, local copies, waits for them, and re-layouts: 5.43 us -> none  [the longest x2 4.2 us: shards(): sources = pairs[owners[tile_cols[0]] // 2]]
  transfers between devices with their start and end apart: 4 -> 1, of which waited for: 3 -> 1; matrix products, arithmetic and copies ran while one was open for 3% -> 0% of each run, Pallas kernels for 0% -> 0%
where the time goes in v1:
time: 106 us; the launch traced here: 105 us
  Pallas kernels  61.7 us (58%)
  waiting for transfers between devices  25.2 us (24%)
  local copies, waits for them, and re-layouts  8.15 us (8%)
  matrix products  4.96 us (5%)
  starting transfers between devices  3.61 us (3%)
    pallas_call x1, Pallas kernels, gather_sources(): pl.pallas_call(gather_kernel, out_shape=jax.ShapeDtypeStruct((4, 16, 8, 1...  56 us
    all_to_all x1, waiting for transfers between devices, copy_for_each(): lax.all_to_all(jnp.broadcast_to(value[None], (devices, *value.shape)), ax...  25.2 us
    unnamed x30, local copies, waits for them, and re-layouts  6.54 us
    pallas_call x1, Pallas kernels, spread_rows(): pl.pallas_call(spread_kernel, out_shape=jax.ShapeDtypeStruct((16, 128, 12...  5.7 us
    all_to_all x1, starting transfers between devices, copy_for_each(): lax.all_to_all(jnp.broadcast_to(value[None], (devices, *value.shape)), ax...  3.61 us
    dot_general x1, matrix products, merge_behaviors(): jnp.dot(hidden, w_down, preferred_element_type=jnp.float32)  2.56 us
  transfers between devices with their start and end apart: 1, of which 1 were waited for; matrix products, arithmetic and copies ran while one was open for 0% of the time, Pallas kernels for 0%

profile of v1, /device:TPU:1, one launch (start us, length us, event | category | flops | bytes accessed | tf_op | source)
XLA Modules:
  0.0 104.8 jit_solution(5596519377488993494)
XLA Ops:
  0.0 0.0 copy-start
  0.7 0.0 copy-start.2
  0.7 1.0 copy-done.2
  1.7 0.7 copy-done.6
  2.4 56.0 %gather_sources.1 = bf16[4,16,8,16,128]{4,3,2,1,0:T(8,128)(2,1)S(1)} custom-call(bf16[16,8,16,128]{3,2,1,0:T(8,128)(2,1)S(1)} %bitcast.49, s32[1,64]{1,0:T(1,128)S(1)} %copy-done.6), custom_call_target="tpu_custom_call" | custom-call | tf_op jit(solution)/shard_map/gather_sources/pallas_call | solution.py:180
  58.4 0.0 copy-start.1
  58.4 2.0 %copy-done.1 = bf16[1,112,128,128]{3,2,1,0:T(8,128)(2,1)S(1)} copy-done((bf16[1,112,128,128]{3,2,1,0:T(8,128)(2,1)S(1)}, bf16[1,112,128,128]{3,2,1,0:T(8,128)(2,1)}, u32[]{:S(2)}) %copy-start.1) | copy-done | bytes 3670040
  60.4 1.0 copy-done.3
  61.4 0.7 copy-done.4
  62.1 0.7 copy-done.5
  62.8 5.7 %spread_rows.1 = bf16[16,128,128]{2,1,0:T(8,128)(2,1)S(1)} custom-call(s32[1,112]{1,0:T(1,128)S(1)} %copy-done.4, s32[1,112]{1,0:T(1,128)S(1)} %copy-done.5, s32[1,1]{1,0:T(1,128)S(6)} %copy.55.count_ref, bf16[64,128,128]{2,1,0:T(8,128)(2,1)S(1)} %bitcast.46, bf16[16,128,128]{2,1,0:T(8,128)(2,1)S(1)} %bitcast.50, bf16[112,128,128]{2,1,0:T(8,128)(2,1)S(1)} %bitcast.47), custom_call_target="tpu_custom_call" | custom-call | tf_op jit(solution)/shard_map/spread_rows/pallas_call | solution.py:252
  68.5 0.0 copy-start.8
  68.5 0.0 copy-start.9
  68.5 0.0 copy-start.10
  68.5 1.6 %broadcast_in_dim.5 = bf16[4,1,2048,128]{3,2,1,0:T(8,128)(2,1)} broadcast(bf16[2048,128]{1,0:T(8,128)(2,1)S(1)} %bitcast.48), dimensions={2,3} | broadcast | bytes 2621440 | tf_op jit(solution)/shard_map/broadcast_in_dim | solution.py:276
  70.1 3.6 %all-to-all-start = ((bf16[4,1,2048,128]{3,2,1,0:T(8,128)(2,1)}), bf16[4,1,2048,128]{3,2,1,0:T(8,128)(2,1)S(1)}, u32[]{:S(2)}, u32[]{:S(2)}) async-start(bf16[4,1,2048,128]{3,2,1,0:T(8,128)(2,1)} %broadcast_in_dim.5), calls=%async_computation | async-start | bytes 4194304 | tf_op jit(solution)/shard_map/all_to_all | solution.py:275
  73.7 0.1 copy.29
  73.9 0.0 copy-done.9
  73.9 0.1 copy.28
  74.0 0.1 copy.27
  74.1 25.2 %all-to-all-done = bf16[4,1,2048,128]{3,2,1,0:T(8,128)(2,1)S(1)} async-done(((bf16[4,1,2048,128]{3,2,1,0:T(8,128)(2,1)}), bf16[4,1,2048,128]{3,2,1,0:T(8,128)(2,1)S(1)}, u32[]{:S(2)}, u32[]{:S(2)}) %all-to-all-start) | async-done | bytes 2097184 | tf_op jit(solution)/shard_map/all_to_all | solution.py:275
  99.3 0.3 fusion.7
  99.6 0.8 multiply_reduce_fusion.1
  100.5 0.0 copy-start.7
  100.5 0.2 fusion.19
  100.7 0.1 copy.47
  100.8 0.0 copy-start.11
  100.8 0.0 copy-start.12
  100.9 0.7 multiply_reduce_fusion
  101.6 0.0 copy-done.7
  101.6 0.6 multiply_reduce_fusion.2
  102.2 2.6 %fusion.2 = bf16[1,2048,128]{2,1,0:T(8,128)(2,1)} fusion(f32[2048,128]{1,0:T(8,128)S(1)} %get-tuple-element.8, bf16[512,128]{1,0:T(8,128)(2,1)S(1)} %copy-done, bf16[128,512]{1,0:T(8,128)(2,1)S(1)} %copy-done.11, f32[128]{0:T(128)S(1)} %copy-done.12, f32[2048]{0:T(1024)S(1)} %add_rsqrt_fusion), kind=kOutput, calls=%fused_computation.7 | convolution fusion | flops 543424512 | bytes 1843712 | tf_op jit(solution)/shard_map/dot_general | solution.py:314
  (11 shorter events, 0.1 us)
Async XLA Ops:
  0.0 102.2 %copy-start = (bf16[512,128]{1,0:T(8,128)(2,1)S(1)}, bf16[512,128]{1,0:T(8,128)(2,1)}, u32[]{:S(2)}) copy-start(bf16[512,128]{1,0:T(8,128)(2,1)} %param.25) | copy-start | bytes 393220
  0.7 1.0 copy-start.2
  1.7 0.7 copy-start.6
  58.4 2.0 %copy-start.1 = (bf16[1,112,128,128]{3,2,1,0:T(8,128)(2,1)S(1)}, bf16[1,112,128,128]{3,2,1,0:T(8,128)(2,1)}, u32[]{:S(2)}) copy-start(bf16[1,112,128,128]{3,2,1,0:T(8,128)(2,1)} %param.14) | copy-start | bytes 11010052
  60.4 1.0 copy-start.3
  61.4 0.7 copy-start.4
  62.1 0.7 copy-start.5
  68.5 5.3 %copy-start.8 = (bf16[128,128]{1,0:T(8,128)(2,1)S(1)}, bf16[128,128]{1,0:T(8,128)(2,1)}, u32[]{:S(2)}) copy-start(bf16[128,128]{1,0:T(8,128)(2,1)} %param.19) | copy-start | bytes 98308
  68.5 5.4 %copy-start.9 = (bf16[128,128]{1,0:T(8,128)(2,1)S(1)}, bf16[128,128]{1,0:T(8,128)(2,1)}, u32[]{:S(2)}) copy-start(bf16[128,128]{1,0:T(8,128)(2,1)} %param.20) | copy-start | bytes 98308
  68.5 5.5 %copy-start.10 = (bf16[128,128]{1,0:T(8,128)(2,1)S(1)}, bf16[128,128]{1,0:T(8,128)(2,1)}, u32[]{:S(2)}) copy-start(bf16[128,128]{1,0:T(8,128)(2,1)} %param.21) | copy-start | bytes 98308
  70.1 29.2 %all-to-all-start = ((bf16[4,1,2048,128]{3,2,1,0:T(8,128)(2,1)}), bf16[4,1,2048,128]{3,2,1,0:T(8,128)(2,1)S(1)}, u32[]{:S(2)}, u32[]{:S(2)}) async-start(bf16[4,1,2048,128]{3,2,1,0:T(8,128)(2,1)} %broadcast_in_dim.5), calls=%async_computation | async-start | bytes 4194304 | tf_op jit(solution)/shard_map/all_to_all | solution.py:275
  100.5 1.1 %copy-start.7 = (bf16[128,128]{1,0:T(8,128)(2,1)S(1)}, bf16[128,128]{1,0:T(8,128)(2,1)}, u32[]{:S(2)}) copy-start(bf16[128,128]{1,0:T(8,128)(2,1)} %param.22) | copy-start | bytes 98308
  100.8 1.4 %copy-start.11 = (bf16[128,512]{1,0:T(8,128)(2,1)S(1)}, bf16[128,512]{1,0:T(8,128)(2,1)}, u32[]{:S(2)}) copy-start(bf16[128,512]{1,0:T(8,128)(2,1)} %param.24) | copy-start | bytes 393220
  100.8 1.4 %copy-start.12 = (f32[128]{0:T(128)S(1)}, f32[128]{0:T(128)}, u32[]{:S(2)}) copy-start(f32[128]{0:T(128)} %param.23) | copy-start | bytes 1540

commit v2 on v1

v2 whole, which is shorter than its diff:
```python
import functools
import math

import jax
import jax.numpy as jnp
from jax import lax
from jax.experimental import pallas as pl
from jax.experimental.pallas import tpu as pltpu
from jax.sharding import PartitionSpec as P

HEAD = 32
MESH = pl.DeviceIdType.MESH
STEPS = 8


def place():
    y = lax.axis_index("beh")
    n = lax.axis_index("node")
    return n // 32, y, lax.rem(n // 2, 16), lax.rem(n, 2)


def device(x, y, z, k):
    return (y, (x * 16 + z) * 2 + k)


def gather_kernel(emb_ref, need_ref, out_ref, *scratch):
    chunks = scratch[:9]
    picked, need_v, need_s = scratch[9:12]
    own_sem, pair_send, pair_recv, ring_send, ring_recv = scratch[12:17]
    ask_send, ask_recv, smem_sem, xy_send, xy_recv = scratch[17:]
    x, y, z, k = place()
    me = x * 8 + y * 2 + k
    part = y * 2 + k
    above = device(x, y, lax.rem(z + 1, 16), k)
    below = device(x, y, lax.rem(z + 15, 16), k)
    twin = device(x, y, z, 1 - k)

    def reader(r):
        return device(r // 8, lax.rem(r, 8) // 2, z, lax.rem(r, 2))

    own = pltpu.make_async_copy(
        emb_ref.at[:, part], chunks[0].at[pl.ds(k * 16, 16)], own_sem
    )
    own.start()

    barrier = pltpu.get_barrier_semaphore()

    @pl.loop(1, 32)
    def _(i):
        pl.semaphore_signal(
            barrier, inc=1, device_id=reader(lax.rem(me + i, 32)), device_id_type=MESH
        )

    for neighbour in (above, below):
        pl.semaphore_signal(barrier, inc=1, device_id=neighbour, device_id_type=MESH)
    pl.semaphore_wait(barrier, 33)

    def half(step, way, h):
        blocks = pl.ds((k + h - 2 * k * h) * 16, 16)
        if step == 0 or step == STEPS:
            return chunks[step].at[blocks]
        return chunks[step].at[way, blocks]

    def hop(step, way, h):
        return pltpu.make_async_remote_copy(
            src_ref=half(step, way, h),
            dst_ref=half(step + 1, way, h),
            send_sem=ring_send.at[way, step, h],
            recv_sem=ring_recv.at[way, step, h],
            device_id=above if way == 0 else below,
            device_id_type=MESH,
        )

    hops = {}

    def forward(step, h):
        for way in range(2):
            if step > 0:
                hops[(step - 1, way, h)].wait_recv()
            if step < STEPS - 1 or way == h:
                hops[(step, way, h)] = hop(step, way, h)
                hops[(step, way, h)].start()

    def pick(step):
        @pl.loop(0, 32)
        def _(r):
            if step == 0:
                index = lax.rem(need_s[r, 0, x * 16 + z], 32)
                picked[r, 0] = chunks[0][index]
            elif step == STEPS:
                index = lax.rem(need_s[r, 0, x * 16 + lax.rem(z + 8, 16)], 32)
                picked[r, 15] = chunks[STEPS][index]
            else:
                index = lax.rem(need_s[r, 0, x * 16 + lax.rem(z + 16 - step, 16)], 32)
                picked[r, 2 * step - 1] = chunks[step][0, index]
                index = lax.rem(need_s[r, 0, x * 16 + lax.rem(z + step, 16)], 32)
                picked[r, 2 * step] = chunks[step][1, index]

    def deliver(step):
        if step == 0:
            slots = pl.ds(0, 1)
        elif step == STEPS:
            slots = pl.ds(15, 1)
        else:
            slots = pl.ds(2 * step - 1, 2)

        @pl.loop(1, 32)
        def _(i):
            r = lax.rem(me + i, 32)
            pltpu.make_async_remote_copy(
                src_ref=picked.at[r, slots],
                dst_ref=out_ref.at[x, slots, part],
                send_sem=xy_send,
                recv_sem=xy_recv,
                device_id=reader(r),
                device_id_type=MESH,
            ).start()

        pltpu.make_async_copy(
            picked.at[me, slots], out_ref.at[x, slots, part], xy_recv
        ).start()

    pair = pltpu.make_async_remote_copy(
        src_ref=emb_ref.at[:, y * 2 + 1 - k],
        dst_ref=chunks[0].at[pl.ds(k * 16, 16)],
        send_sem=pair_send,
        recv_sem=pair_recv,
        device_id=twin,
        device_id_type=MESH,
    )
    pair.start()

    own.wait()
    forward(0, 0)
    @pl.loop(1, 32)
    def _(i):
        pltpu.make_async_remote_copy(
            src_ref=need_ref,
            dst_ref=need_v.at[me],
            send_sem=ask_send,
            recv_sem=ask_recv,
            device_id=reader(lax.rem(me + i, 32)),
            device_id_type=MESH,
        ).start()

    pltpu.make_async_copy(need_ref, need_v.at[me], ask_recv).start()

    pair.wait_recv()
    forward(0, 1)
    forward(1, 0)
    pltpu.make_async_copy(need_v, need_v, ask_recv).wait()
    table = pltpu.make_async_copy(need_v, need_s, smem_sem)
    table.start()
    table.wait()
    pick(0)
    deliver(0)
    for step in range(1, STEPS):
        if step > 1:
            forward(step, 0)
        forward(step, 1)
        pick(step)
        deliver(step)
    hops[(STEPS - 1, 0, 0)].wait_recv()
    hops[(STEPS - 1, 1, 1)].wait_recv()
    pick(STEPS)
    deliver(STEPS)

    pair.wait_send()
    for one in hops.values():
        one.wait_send()
    asked = need_v.at[pl.ds(0, 31)]
    pltpu.make_async_copy(asked, asked, ask_send).wait()
    sent = picked.at[pl.ds(0, 31)]
    pltpu.make_async_copy(sent, sent, xy_send).wait()
    pltpu.make_async_copy(out_ref, out_ref, xy_recv).wait()


def gather_sources(embeddings, need):
    dma = pltpu.SemaphoreType.DMA
    one = pltpu.VMEM((32, 16, 128), jnp.bfloat16)
    two = pltpu.VMEM((2, 32, 16, 128), jnp.bfloat16)
    return pl.pallas_call(
        gather_kernel,
        out_shape=jax.ShapeDtypeStruct((4, 16, 8, 16, 128), jnp.bfloat16),
        in_specs=[pl.BlockSpec(memory_space=pltpu.HBM)] * 2,
        out_specs=pl.BlockSpec(memory_space=pltpu.VMEM),
        scratch_shapes=[
            one,
            *([two] * 7),
            one,
            pltpu.VMEM((32, 16, 16, 128), jnp.bfloat16),
            pltpu.VMEM((32, 1, 64), jnp.int32),
            pltpu.SMEM((32, 1, 64), jnp.int32),
            dma,
            dma,
            dma,
            dma((2, 8, 2)),
            dma((2, 8, 2)),
            dma,
            dma,
            dma,
            dma,
            dma,
        ],
        compiler_params=pltpu.CompilerParams(
            collective_id=0, has_side_effects=True, vmem_limit_bytes=16 * 2**20
        ),
        cost_estimate=pl.CostEstimate(
            flops=2**33, transcendentals=0, bytes_accessed=2**26
        ),
        name="gather_sources",
    )(
        pltpu.with_memory_space_constraint(embeddings.reshape(16, 8, 16, 128), pltpu.HBM),
        pltpu.with_memory_space_constraint(need, pltpu.HBM),
    )


GROUP = 4
TILES = 112


def spread_kernel(rows_ref, cols_ref, count_ref, src_ref, emb_ref, adj_ref, out_ref, acc):
    z = place()[2]
    count = count_ref[0, 0]

    acc[0:16] = emb_ref[...].astype(jnp.float32)

    def add(t):
        col = cols_ref[0, t]
        away = lax.rem(lax.rem(col, 16) - z + 16, 16)
        slot = jnp.where(away < 8, 2 * away, jnp.where(away == 8, 15, 31 - 2 * away))
        row = jnp.where(t < count, rows_ref[0, t], 16)
        product = jnp.dot(
            adj_ref[t], src_ref[(col // 16) * 16 + slot], preferred_element_type=jnp.float32
        )
        acc[row] += product

    @pl.loop(0, (count + GROUP - 1) // GROUP)
    def _(i):
        for j in range(GROUP):
            add(i * GROUP + j)

    out_ref[...] = acc[0:16].astype(jnp.bfloat16)


def spread_rows(rows, cols, count, sources, embeddings, adjacency):
    smem = pl.BlockSpec(memory_space=pltpu.SMEM)
    vmem = pl.BlockSpec(memory_space=pltpu.VMEM)
    return pl.pallas_call(
        spread_kernel,
        out_shape=jax.ShapeDtypeStruct((16, 128, 128), jnp.bfloat16),
        in_specs=[smem, smem, smem, vmem, vmem, vmem],
        out_specs=vmem,
        scratch_shapes=[
            pltpu.VMEM((17, 128, 128), jnp.float32),
        ],
        compiler_params=pltpu.CompilerParams(vmem_limit_bytes=20 * 2**20),
        name="spread_rows",
    )(rows, cols, count, sources.reshape(64, 128, 128), embeddings.reshape(16, 128, 128), adjacency)


CHUNKS = 4
ROWS = 512 // CHUNKS


def merge_kernel(
    spread_ref,
    wq_ref,
    wk_ref,
    wv_ref,
    wo_ref,
    gain_ref,
    up_ref,
    down_ref,
    out_ref,
    got,
    done,
    own_sem,
    in_send,
    in_recv,
    out_send,
    out_recv,
):
    x, y, z, k = place()
    own = pltpu.make_async_copy(spread_ref.at[y], got.at[y], own_sem)
    own.start()
    barrier = pltpu.get_barrier_semaphore()
    for i in range(1, 4):
        pl.semaphore_signal(
            barrier, inc=1, device_id=device(x, lax.rem(y + i, 4), z, k), device_id_type=MESH
        )
    pl.semaphore_wait(barrier, 3)

    @pl.loop(0, CHUNKS)
    def _(c):
        span = pl.ds(pl.multiple_of(c * ROWS, ROWS), ROWS)
        for i in range(1, 4):
            there = lax.rem(y + i, 4)
            pltpu.make_async_remote_copy(
                src_ref=spread_ref.at[there, span],
                dst_ref=got.at[y, span],
                send_sem=in_send,
                recv_sem=in_recv.at[c],
                device_id=device(x, there, z, k),
                device_id_type=MESH,
            ).start()

    lane = lax.broadcasted_iota(jnp.int32, (128, 128), 0) // HEAD
    same = (lane == lax.broadcasted_iota(jnp.int32, (128, 128), 1) // HEAD).astype(jnp.bfloat16)
    own.wait()

    @pl.loop(0, CHUNKS)
    def _(c):
        span = pl.ds(pl.multiple_of(c * ROWS, ROWS), ROWS)
        arrived = got.at[pl.ds(0, 3), span]
        pltpu.make_async_copy(arrived, arrived, in_recv.at[c]).wait()
        flat = got[:, span, :].reshape(4 * ROWS, 128)
        query = jnp.dot(flat, wq_ref[...], preferred_element_type=jnp.float32)
        query = query * (math.log2(math.e) / math.sqrt(HEAD))
        key = jnp.dot(flat, wk_ref[...], preferred_element_type=jnp.float32)
        value = jnp.dot(flat, wv_ref[...], preferred_element_type=jnp.float32)
        mixed = []
        for q in range(4):
            mine = query[q * ROWS : (q + 1) * ROWS]
            scores = []
            for b in range(4):
                part = mine * key[b * ROWS : (b + 1) * ROWS]
                high = part.astype(jnp.bfloat16)
                low = (part - high.astype(jnp.float32)).astype(jnp.bfloat16)
                scores.append(
                    jnp.dot(high, same, preferred_element_type=jnp.float32)
                    + jnp.dot(low, same, preferred_element_type=jnp.float32)
                )
            top = jnp.maximum(
                jnp.maximum(scores[0], scores[1]), jnp.maximum(scores[2], scores[3])
            )
            weights = [jnp.exp2(s - top) for s in scores]
            total = (weights[0] + weights[1]) + (weights[2] + weights[3])
            blend = weights[0] * value[:ROWS]
            for b in range(1, 4):
                blend = blend + weights[b] * value[b * ROWS : (b + 1) * ROWS]
            mixed.append((blend / total).astype(jnp.bfloat16))
        mixture = jnp.concatenate(mixed, axis=0)
        residual = flat.astype(jnp.float32) + jnp.dot(
            mixture, wo_ref[...], preferred_element_type=jnp.float32
        )
        meansq = jnp.mean(residual * residual, axis=-1, keepdims=True)
        normed = (residual * lax.rsqrt(meansq + 1e-06) * gain_ref[...]).astype(jnp.bfloat16)
        hidden = jax.nn.silu(
            jnp.dot(normed, up_ref[...], preferred_element_type=jnp.float32)
        ).astype(jnp.bfloat16)
        result = residual + jnp.dot(hidden, down_ref[...], preferred_element_type=jnp.float32)
        done[:, span, :] = result.astype(jnp.bfloat16).reshape(4, ROWS, 128)
        for i in range(1, 4):
            there = lax.rem(y + i, 4)
            pltpu.make_async_remote_copy(
                src_ref=done.at[there, span],
                dst_ref=out_ref.at[y, span],
                send_sem=out_send,
                recv_sem=out_recv,
                device_id=device(x, there, z, k),
                device_id_type=MESH,
            ).start()

    own = pltpu.make_async_copy(done.at[y], out_ref.at[y], own_sem)
    own.start()
    own.wait()
    three = got.at[pl.ds(0, 3)]
    pltpu.make_async_copy(three, three, in_send).wait()
    pltpu.make_async_copy(three, three, out_send).wait()
    pltpu.make_async_copy(three, three, out_recv).wait()


def merge_rows(spread, w_query, w_key, w_value, w_out, mlp_gain, w_up, w_down):
    dma = pltpu.SemaphoreType.DMA
    vmem = pl.BlockSpec(memory_space=pltpu.VMEM)
    quarters = (4, 512, 128)
    return pl.pallas_call(
        merge_kernel,
        out_shape=jax.ShapeDtypeStruct(quarters, jnp.bfloat16),
        in_specs=[vmem] * 8,
        out_specs=vmem,
        scratch_shapes=[
            pltpu.VMEM(quarters, jnp.bfloat16),
            pltpu.VMEM(quarters, jnp.bfloat16),
            dma,
            dma,
            dma((CHUNKS,)),
            dma,
            dma,
        ],
        compiler_params=pltpu.CompilerParams(
            collective_id=1, has_side_effects=True, vmem_limit_bytes=24 * 2**20
        ),
        name="merge_rows",
    )(
        spread.reshape(quarters),
        w_query,
        w_key,
        w_value,
        w_out,
        mlp_gain.reshape(1, 128),
        w_up,
        w_down,
    )


def shards(
    embeddings,
    adjacency,
    tile_rows,
    tile_cols,
    tile_count,
    need_ids,
    w_query,
    w_key,
    w_value,
    w_out,
    mlp_gain,
    w_up,
    w_down,
):
    sources = gather_sources(embeddings, need_ids)
    spread = spread_rows(tile_rows, tile_cols, tile_count, sources, embeddings, adjacency[0])
    merged = merge_rows(spread, w_query, w_key, w_value, w_out, mlp_gain, w_up, w_down)
    return merged.reshape(1, *embeddings.shape)


def solution(mesh):
    in_specs = (
        P("node", None),
        P("beh", "node", None, None),
        P("beh", "node"),
        P("beh", "node"),
        P("beh", "node"),
        P("beh", "node"),
        P(),
        P(),
        P(),
        P(),
        P(),
        P(),
        P(),
    )
    out_specs = P("beh", "node", None)
    return jax.shard_map(shards, mesh=mesh, in_specs=in_specs, out_specs=out_specs, check_vma=False)
```

time: 106 us -> 79.3 us (0.75)
  waiting for transfers between devices: 25.2 us -> 0 us
  Pallas kernels: 61.7 us -> 77.3 us
  local copies, waits for them, and re-layouts: 8.15 us -> 0.86 us
  matrix products: 4.96 us -> 0 us
  starting transfers between devices: 3.61 us -> 0 us
    all_to_all x1 -> x0, waiting for transfers between devices: 25.2 us -> none  [copy_for_each(): lax.all_to_all(jnp.broadcast_to(value[None], (devices, *value.shape)), ax...]
    pallas_call x0 -> x1, Pallas kernels: none -> 15.9 us  [merge_rows(): pl.pallas_call(merge_kernel, out_shape=jax.ShapeDtypeStruct(quarters, jnp...]
    unnamed x30 -> x23, local copies, waits for them, and re-layouts: 6.54 us -> 0.86 us
    dot_general x5 -> x0, matrix products: 4.96 us -> none  [the longest x1 2.56 us: merge_behaviors(): jnp.dot(hidden, w_down, preferred_element_type=jnp.float32)]
    all_to_all x1 -> x0, starting transfers between devices: 3.61 us -> none  [copy_for_each(): lax.all_to_all(jnp.broadcast_to(value[None], (devices, *value.shape)), ax...]
    broadcast_in_dim x1 -> x0, local copies, waits for them, and re-layouts: 1.61 us -> none  [copy_for_each(): jnp.broadcast_to(value[None], (devices, *value.shape))]
  transfers between devices with their start and end apart: 1 -> 0, of which waited for: 1 -> 0; matrix products, arithmetic and copies ran while one was open for 0% -> 0% of each run, Pallas kernels for 0% -> 0%
where the time goes in v2:
time: 79.3 us; the launch traced here: 79 us
  Pallas kernels  77.3 us (97%)
  local copies, waits for them, and re-layouts  0.86 us (1%)
  between operations  0.85 us (1%)
    pallas_call x1, Pallas kernels, gather_sources(): pl.pallas_call(gather_kernel, out_shape=jax.ShapeDtypeStruct((4, 16, 8, 1...  55.7 us
    pallas_call x1, Pallas kernels, merge_rows(): pl.pallas_call(merge_kernel, out_shape=jax.ShapeDtypeStruct(quarters, jnp...  15.9 us
    pallas_call x1, Pallas kernels, spread_rows(): pl.pallas_call(spread_kernel, out_shape=jax.ShapeDtypeStruct((16, 128, 12...  5.63 us

profile of v2, /device:TPU:1, one launch (start us, length us, event | category | flops | bytes accessed | tf_op | source)
XLA Modules:
  0.0 79.0 jit_solution(18017390703581876163)
XLA Ops:
  0.7 0.0 copy-start
  0.7 0.0 copy-start.1
  0.7 0.0 copy-start.8
  0.7 0.0 copy-start.9
  0.7 55.7 %gather_sources.1 = bf16[4,16,8,16,128]{4,3,2,1,0:T(8,128)(2,1)S(1)} custom-call(bf16[16,8,16,128]{3,2,1,0:T(8,128)(2,1)} %bitcast.11, s32[1,64]{1,0:T(1,128)} %need_ref.1), custom_call_target="tpu_custom_call" | custom-call | flops 8589934592 | bytes 67108864 | tf_op jit(solution)/shard_map/gather_sources/pallas_call | solution.py:182
  56.4 0.0 copy-start.2
  56.4 0.0 copy-start.3
  56.5 0.0 copy-start.4
  56.5 0.0 copy-start.5
  56.5 0.0 copy-start.6
  56.5 0.0 copy-start.7
  56.5 0.0 copy-start.10
  56.5 0.0 copy-done
  56.5 0.0 copy-done.1
  56.5 0.0 copy-done.8
  56.5 0.0 copy-done.9
  56.6 5.6 %spread_rows.1 = bf16[16,128,128]{2,1,0:T(8,128)(2,1)S(1)} custom-call(s32[1,112]{1,0:T(1,128)S(1)} %copy-done.8, s32[1,112]{1,0:T(1,128)S(1)} %copy-done.9, s32[1,1]{1,0:T(1,128)S(6)} %copy.15.count_ref, bf16[64,128,128]{2,1,0:T(8,128)(2,1)S(1)} %bitcast.9, bf16[16,128,128]{2,1,0:T(8,128)(2,1)S(1)} %bitcast.12, bf16[112,128,128]{2,1,0:T(8,128)(2,1)S(1)} %bitcast.7), custom_call_target="tpu_custom_call" | custom-call | tf_op jit(solution)/shard_map/spread_rows/pallas_call | solution.py:249
  62.2 0.0 copy-done.2
  62.2 0.0 copy-done.3
  62.2 0.0 copy-done.4
  62.2 0.0 copy-done.5
  62.2 0.0 copy-done.6
  62.2 0.0 copy-done.7
  62.3 0.0 copy-done.10
  62.3 15.9 %merge_rows.1 = bf16[4,512,128]{2,1,0:T(8,128)(2,1)S(1)} custom-call(bf16[4,512,128]{2,1,0:T(8,128)(2,1)S(1)} %bitcast.8, bf16[128,128]{1,0:T(8,128)(2,1)S(1)} %copy-done.4, bf16[128,128]{1,0:T(8,128)(2,1)S(1)} %copy-done.5, bf16[128,128]{1,0:T(8,128)(2,1)S(1)} %copy-done.6, bf16[128,128]{1,0:T(8,128)(2,1)S(1)} %copy-done.7, f32[1,128]{1,0:T(1,128)S(1)} %bitcast.13, ...), custom_call_target="tpu_custom_call" | custom-call | tf_op jit(solution)/shard_map/merge_rows/pallas_call | solution.py:378
  78.2 0.8 %copy.16 = bf16[1,2048,128]{2,1,0:T(8,128)(2,1)} copy(bf16[1,2048,128]{2,1,0:T(8,128)(2,1)S(1)} %bitcast.10) | data formatting | bytes 1048576
Async XLA Ops:
  0.7 55.9 %copy-start = (bf16[1,112,128,128]{3,2,1,0:T(8,128)(2,1)S(1)}, bf16[1,112,128,128]{3,2,1,0:T(8,128)(2,1)}, u32[]{:S(2)}) copy-start(bf16[1,112,128,128]{3,2,1,0:T(8,128)(2,1)} %param.14) | copy-start | bytes 11010052
  0.7 55.9 %copy-start.1 = (bf16[2048,128]{1,0:T(8,128)(2,1)S(1)}, bf16[2048,128]{1,0:T(8,128)(2,1)}, u32[]{:S(2)}) copy-start(bf16[2048,128]{1,0:T(8,128)(2,1)} %param.13) | copy-start | bytes 1572868
  0.7 55.9 %copy-start.8 = (s32[1,112]{1,0:T(1,128)S(1)}, s32[1,112]{1,0:T(1,128)}, u32[]{:S(2)}) copy-start(s32[1,112]{1,0:T(1,128)} %rows_ref.1) | copy-start | bytes 1348
  0.7 55.9 %copy-start.9 = (s32[1,112]{1,0:T(1,128)S(1)}, s32[1,112]{1,0:T(1,128)}, u32[]{:S(2)}) copy-start(s32[1,112]{1,0:T(1,128)} %cols_ref.1) | copy-start | bytes 1348
  56.4 5.8 %copy-start.2 = (bf16[128,512]{1,0:T(8,128)(2,1)S(1)}, bf16[128,512]{1,0:T(8,128)(2,1)}, u32[]{:S(2)}) copy-start(bf16[128,512]{1,0:T(8,128)(2,1)} %up_ref.1) | copy-start | bytes 393220
  56.4 5.8 %copy-start.3 = (bf16[512,128]{1,0:T(8,128)(2,1)S(1)}, bf16[512,128]{1,0:T(8,128)(2,1)}, u32[]{:S(2)}) copy-start(bf16[512,128]{1,0:T(8,128)(2,1)} %down_ref.1) | copy-start | bytes 393220
  56.5 5.8 %copy-start.4 = (bf16[128,128]{1,0:T(8,128)(2,1)S(1)}, bf16[128,128]{1,0:T(8,128)(2,1)}, u32[]{:S(2)}) copy-start(bf16[128,128]{1,0:T(8,128)(2,1)} %wq_ref.1) | copy-start | bytes 98308
  56.5 5.8 %copy-start.5 = (bf16[128,128]{1,0:T(8,128)(2,1)S(1)}, bf16[128,128]{1,0:T(8,128)(2,1)}, u32[]{:S(2)}) copy-start(bf16[128,128]{1,0:T(8,128)(2,1)} %wk_ref.1) | copy-start | bytes 98308
  56.5 5.8 %copy-start.6 = (bf16[128,128]{1,0:T(8,128)(2,1)S(1)}, bf16[128,128]{1,0:T(8,128)(2,1)}, u32[]{:S(2)}) copy-start(bf16[128,128]{1,0:T(8,128)(2,1)} %wv_ref.1) | copy-start | bytes 98308
  56.5 5.8 %copy-start.7 = (bf16[128,128]{1,0:T(8,128)(2,1)S(1)}, bf16[128,128]{1,0:T(8,128)(2,1)}, u32[]{:S(2)}) copy-start(bf16[128,128]{1,0:T(8,128)(2,1)} %wo_ref.1) | copy-start | bytes 98308
  56.5 5.8 %copy-start.10 = (f32[128]{0:T(128)S(1)}, f32[128]{0:T(128)}, u32[]{:S(2)}) copy-start(f32[128]{0:T(128)} %param.23) | copy-start | bytes 1540

commit v3 on v2

--- a/solution.py
+++ b/solution.py
@@ -11,6 +11,10 @@
 HEAD = 32
 MESH = pl.DeviceIdType.MESH
 STEPS = 8
+FAR_FIRST = sorted(
+    ((i, j) for i in range(4) for j in range(8) if i or j),
+    key=lambda at: -(min(at[0], 4 - at[0]) * 2 + min(at[1], 8 - at[1])),
+)
 
 
 def place():
@@ -25,182 +29,182 @@
 
 def gather_kernel(emb_ref, need_ref, out_ref, *scratch):
     chunks = scratch[:9]
-    picked, need_v, need_s = scratch[9:12]
-    own_sem, pair_send, pair_recv, ring_send, ring_recv = scratch[12:17]
-    ask_send, ask_recv, smem_sem, xy_send, xy_recv = scratch[17:]
+    picked, mid, need_x, need_v, need_s = scratch[9:14]
+    own_sem, pair_send, pair_recv, ring_send, ring_recv = scratch[14:19]
+    ask_send, ask_recv, smem_sem, x_send, x_recv, y_send, y_recv = scratch[19:]
     x, y, z, k = place()
-    me = x * 8 + y * 2 + k
     part = y * 2 + k
     above = device(x, y, lax.rem(z + 1, 16), k)
     below = device(x, y, lax.rem(z + 15, 16), k)
     twin = device(x, y, z, 1 - k)
-
-    def reader(r):
-        return device(r // 8, lax.rem(r, 8) // 2, z, lax.rem(r, 2))
+    rows = [lax.rem(x + i, 4) for i in range(4)]
+    parts = [lax.rem(part + i, 8) for i in range(8)]
+    row_peers = [device(xx, y, z, k) for xx in rows]
+    part_peers = [device(x, p // 2, z, lax.rem(p, 2)) for p in parts]
+
+    def send(src, dst, sent, landed, where):
+        copy = pltpu.make_async_remote_copy(
+            src_ref=src,
+            dst_ref=dst,
+            send_sem=sent,
+            recv_sem=landed,
+            device_id=where,
+            device_id_type=MESH,
+        )
+        copy.start()
+        return copy
+
+    def wait_bytes(ref, sem):
+        pltpu.make_async_copy(ref, ref, sem).wait()
 
     own = pltpu.make_async_copy(
         emb_ref.at[:, part], chunks[0].at[pl.ds(k * 16, 16)], own_sem
     )
     own.start()
+    pltpu.make_async_copy(need_ref, need_x.at[x], ask_recv.at[0]).start()
 
     barrier = pltpu.get_barrier_semaphore()
-
-    @pl.loop(1, 32)
-    def _(i):
-        pl.semaphore_signal(
-            barrier, inc=1, device_id=reader(lax.rem(me + i, 32)), device_id_type=MESH
-        )
-
-    for neighbour in (above, below):
-        pl.semaphore_signal(barrier, inc=1, device_id=neighbour, device_id_type=MESH)
-    pl.semaphore_wait(barrier, 33)
+    for peer in (above, below, *row_peers[1:], *part_peers[1:]):
+        pl.semaphore_signal(barrier, inc=1, device_id=peer, device_id_type=MESH)
+    pl.semaphore_wait(barrier, 12)
 
     def half(step, way, h):
-        blocks = pl.ds((k + h - 2 * k * h) * 16, 16)
+        core = k if h < 2 else 1 - k
+        blocks = pl.ds(core * 16 + (h % 2) * 8, 8)
         if step == 0 or step == STEPS:
             return chunks[step].at[blocks]
         return chunks[step].at[way, blocks]
 
-    def hop(step, way, h):
-        return pltpu.make_async_remote_copy(
-            src_ref=half(step, way, h),
-            dst_ref=half(step + 1, way, h),
-            send_sem=ring_send.at[way, step, h],
-            recv_sem=ring_recv.at[way, step, h],
-            device_id=above if way == 0 else below,
-            device_id_type=MESH,
-        )
-
     hops = {}
 
     def forward(step, h):
         for way in range(2):
-            if step > 0:
+            if (step - 1, way, h) in hops:
                 hops[(step - 1, way, h)].wait_recv()
-            if step < STEPS - 1 or way == h:
-                hops[(step, way, h)] = hop(step, way, h)
-                hops[(step, way, h)].start()
-
-    def pick(step):
-        @pl.loop(0, 32)
-        def _(r):
-            if step == 0:
-                index = lax.rem(need_s[r, 0, x * 16 + z], 32)
-                picked[r, 0] = chunks[0][index]
-            elif step == STEPS:
-                index = lax.rem(need_s[r, 0, x * 16 + lax.rem(z + 8, 16)], 32)
-                picked[r, 15] = chunks[STEPS][index]
-            else:
-                index = lax.rem(need_s[r, 0, x * 16 + lax.rem(z + 16 - step, 16)], 32)
-                picked[r, 2 * step - 1] = chunks[step][0, index]
-                index = lax.rem(need_s[r, 0, x * 16 + lax.rem(z + step, 16)], 32)
-                picked[r, 2 * step] = chunks[step][1, index]
+            if step < STEPS - 1 or (step < STEPS and way == h % 2):
+                hops[(step, way, h)] = send(
+                    half(step, way, h),
+                    half(step + 1, way, h),
+                    ring_send.at[way, step, h],
+                    ring_recv.at[way, step, h],
+                    above if way == 0 else below,
+                )
+
+    def third(step):
+        return 0 if step == 0 else 2 if step == STEPS else 1
+
+    def pick(step, low=0, high=8):
+        @pl.loop(low, high)
+        def _(p):
+            for xx in range(4):
+                if step == 0:
+                    index = lax.rem(need_s[p, xx, 0, x * 16 + z], 32)
+                    picked[0, xx * 8 + p, 0] = chunks[0][index]
+                elif step == STEPS:
+                    index = lax.rem(need_s[p, xx, 0, x * 16 + lax.rem(z + 8, 16)], 32)
+                    picked[STEPS, xx * 8 + p, 0] = chunks[STEPS][index]
+                else:
+                    index = lax.rem(need_s[p, xx, 0, x * 16 + lax.rem(z + 16 - step, 16)], 32)
+                    picked[step, xx * 8 + p, 0] = chunks[step][0, index]
+                    index = lax.rem(need_s[p, xx, 0, x * 16 + lax.rem(z + step, 16)], 32)
+                    picked[step, xx * 8 + p, 1] = chunks[step][1, index]
+
+    me = x * 8 + part
 
     def deliver(step):
-        if step == 0:
-            slots = pl.ds(0, 1)
-        elif step == STEPS:
-            slots = pl.ds(15, 1)
-        else:
-            slots = pl.ds(2 * step - 1, 2)
-
-        @pl.loop(1, 32)
-        def _(i):
-            r = lax.rem(me + i, 32)
-            pltpu.make_async_remote_copy(
-                src_ref=picked.at[r, slots],
-                dst_ref=out_ref.at[x, slots, part],
-                send_sem=xy_send,
-                recv_sem=xy_recv,
-                device_id=reader(r),
-                device_id_type=MESH,
-            ).start()
-
+        width = pl.ds(0, 1 if step == 0 or step == STEPS else 2)
+        turn = third(step)
         pltpu.make_async_copy(
-            picked.at[me, slots], out_ref.at[x, slots, part], xy_recv
+            picked.at[step, me, width], out_ref.at[step, part, x, width], y_recv.at[turn]
         ).start()
-
-    pair = pltpu.make_async_remote_copy(
-        src_ref=emb_ref.at[:, y * 2 + 1 - k],
-        dst_ref=chunks[0].at[pl.ds(k * 16, 16)],
-        send_sem=pair_send,
-        recv_sem=pair_recv,
-        device_id=twin,
-        device_id_type=MESH,
+        for i, j in FAR_FIRST:
+            send(
+                picked.at[step, rows[i] * 8 + parts[j], width],
+                out_ref.at[step, part, x, width],
+                y_send.at[turn],
+                y_recv.at[turn],
+                device(rows[i], parts[j] // 2, z, lax.rem(parts[j], 2)),
+            )
+
+    for peer in row_peers[1:]:
+        send(need_ref, need_x.at[x], ask_send.at[0], ask_recv.at[0], peer)
+    pair = send(
+        emb_ref.at[:, y * 2 + 1 - k],
+        chunks[0].at[pl.ds(k * 16, 16)],
+        pair_send,
+        pair_recv,
+        twin,
     )
-    pair.start()
-
     own.wait()
     forward(0, 0)
-    @pl.loop(1, 32)
-    def _(i):
-        pltpu.make_async_remote_copy(
-            src_ref=need_ref,
-            dst_ref=need_v.at[me],
-            send_sem=ask_send,
-            recv_sem=ask_recv,
-            device_id=reader(lax.rem(me + i, 32)),
-            device_id_type=MESH,
-        ).start()
-
-    pltpu.make_async_copy(need_ref, need_v.at[me], ask_recv).start()
-
+    forward(0, 1)
+    wait_bytes(need_x, ask_recv.at[0])
+    for peer in part_peers[1:]:
+        send(need_x, need_v.at[part], ask_send.at[1], ask_recv.at[1], peer)
+    pltpu.make_async_copy(need_x, need_v.at[part], ask_recv.at[1]).start()
     pair.wait_recv()
-    forward(0, 1)
+    forward(0, 2)
+    forward(0, 3)
     forward(1, 0)
-    pltpu.make_async_copy(need_v, need_v, ask_recv).wait()
+    forward(1, 1)
+    wait_bytes(need_v, ask_recv.at[1])
     table = pltpu.make_async_copy(need_v, need_s, smem_sem)
     table.start()
+    forward(1, 2)
     table.wait()
+    forward(1, 3)
     pick(0)
     deliver(0)
-    for step in range(1, STEPS):
-        if step > 1:
-            forward(step, 0)
-        forward(step, 1)
+    pick(1)
+    deliver(1)
+    for step in range(2, STEPS + 1):
+        for h in range(4):
+            forward(step, h)
         pick(step)
         deliver(step)
-    hops[(STEPS - 1, 0, 0)].wait_recv()
-    hops[(STEPS - 1, 1, 1)].wait_recv()
-    pick(STEPS)
-    deliver(STEPS)
 
     pair.wait_send()
     for one in hops.values():
         one.wait_send()
-    asked = need_v.at[pl.ds(0, 31)]
-    pltpu.make_async_copy(asked, asked, ask_send).wait()
-    sent = picked.at[pl.ds(0, 31)]
-    pltpu.make_async_copy(sent, sent, xy_send).wait()
-    pltpu.make_async_copy(out_ref, out_ref, xy_recv).wait()
+    wait_bytes(need_x.at[pl.ds(0, 3)], ask_send.at[0])
+    wait_bytes(need_v.at[pl.ds(0, 7)], ask_send.at[1])
+    ends = ((0, pl.ds(0, 1), pl.ds(0, 1)), (1, pl.ds(1, 7), pl.ds(0, 2)), (2, pl.ds(8, 1), pl.ds(0, 1)))
+    for turn, steps, width in ends:
+        wait_bytes(picked.at[steps, pl.ds(0, 31), width], y_send.at[turn])
+        wait_bytes(out_ref.at[steps, :, :, width], y_recv.at[turn])
 
 
 def gather_sources(embeddings, need):
     dma = pltpu.SemaphoreType.DMA
     one = pltpu.VMEM((32, 16, 128), jnp.bfloat16)
     two = pltpu.VMEM((2, 32, 16, 128), jnp.bfloat16)
+    picks = pltpu.VMEM((9, 32, 2, 16, 128), jnp.bfloat16)
     return pl.pallas_call(
         gather_kernel,
-        out_shape=jax.ShapeDtypeStruct((4, 16, 8, 16, 128), jnp.bfloat16),
+        out_shape=jax.ShapeDtypeStruct((9, 8, 4, 2, 16, 128), jnp.bfloat16),
         in_specs=[pl.BlockSpec(memory_space=pltpu.HBM)] * 2,
         out_specs=pl.BlockSpec(memory_space=pltpu.VMEM),
         scratch_shapes=[
             one,
             *([two] * 7),
             one,
-            pltpu.VMEM((32, 16, 16, 128), jnp.bfloat16),
-            pltpu.VMEM((32, 1, 64), jnp.int32),
-            pltpu.SMEM((32, 1, 64), jnp.int32),
-            dma,
-            dma,
-            dma,
-            dma((2, 8, 2)),
-            dma((2, 8, 2)),
-            dma,
-            dma,
-            dma,
-            dma,
-            dma,
+            picks,
+            pltpu.VMEM((8, 128), jnp.float32),
+            pltpu.VMEM((4, 1, 64), jnp.int32),
+            pltpu.VMEM((8, 4, 1, 64), jnp.int32),
+            pltpu.SMEM((8, 4, 1, 64), jnp.int32),
+            dma,
+            dma,
+            dma,
+            dma((2, 8, 4)),
+            dma((2, 8, 4)),
+            dma((2,)),
+            dma((2,)),
+            dma,
+            dma((3,)),
+            dma((9,)),
+            dma((3,)),
+            dma((3,)),
         ],
         compiler_params=pltpu.CompilerParams(
             collective_id=0, has_side_effects=True, vmem_limit_bytes=16 * 2**20
@@ -228,10 +232,11 @@
     def add(t):
         col = cols_ref[0, t]
         away = lax.rem(lax.rem(col, 16) - z + 16, 16)
-        slot = jnp.where(away < 8, 2 * away, jnp.where(away == 8, 15, 31 - 2 * away))
+        step = jnp.minimum(away, 16 - away)
+        way = jnp.where((away > 0) & (away < 8), 1, 0)
         row = jnp.where(t < count, rows_ref[0, t], 16)
         product = jnp.dot(
-            adj_ref[t], src_ref[(col // 16) * 16 + slot], preferred_element_type=jnp.float32
+            adj_ref[t], src_ref[step, :, col // 16, way].reshape(128, 128), preferred_element_type=jnp.float32
         )
         acc[row] += product
 
@@ -256,7 +261,7 @@
         ],
         compiler_params=pltpu.CompilerParams(vmem_limit_bytes=20 * 2**20),
         name="spread_rows",
-    )(rows, cols, count, sources.reshape(64, 128, 128), embeddings.reshape(16, 128, 128), adjacency)
+    )(rows, cols, count, sources, embeddings.reshape(16, 128, 128), adjacency)
 
 
 CHUNKS = 4

time: 79.3 us -> 74 us (0.933)
  Pallas kernels: 77.3 us -> 72.8 us
    pallas_call x1, Pallas kernels: 55.7 us -> 50.7 us  [gather_sources(): pl.pallas_call(gather_kernel, out_shape=jax.ShapeDtypeStruct((9, 8, 4, 2,...]
    pallas_call x1, Pallas kernels: 15.9 us -> 17.1 us  [merge_rows(): pl.pallas_call(merge_kernel, out_shape=jax.ShapeDtypeStruct(quarters, jnp...]
where the time goes in v3:
time: 74 us; the launch traced here: 74.5 us
  Pallas kernels  72.8 us (98%)
  local copies, waits for them, and re-layouts  0.86 us (1%)
  between operations  0.85 us (1%)
    pallas_call x1, Pallas kernels, gather_sources(): pl.pallas_call(gather_kernel, out_shape=jax.ShapeDtypeStruct((9, 8, 4, 2,...  50.7 us
    pallas_call x1, Pallas kernels, merge_rows(): pl.pallas_call(merge_kernel, out_shape=jax.ShapeDtypeStruct(quarters, jnp...  17.1 us
    pallas_call x1, Pallas kernels, spread_rows(): pl.pallas_call(spread_kernel, out_shape=jax.ShapeDtypeStruct((16, 128, 12...  4.91 us

profile of v3, /device:TPU:1, one launch (start us, length us, event | category | flops | bytes accessed | tf_op | source)
XLA Modules:
  0.0 74.5 jit_solution(6345425426239455163)
XLA Ops:
  0.7 0.0 copy-start
  0.7 0.0 copy-start.1
  0.7 0.0 copy-start.8
  0.7 0.0 copy-start.9
  0.7 50.7 %gather_sources.1.src_ref = bf16[9,8,4,2,16,128]{5,4,3,2,1,0:T(8,128)(2,1)S(1)} custom-call(bf16[16,8,16,128]{3,2,1,0:T(8,128)(2,1)} %bitcast.9, s32[1,64]{1,0:T(1,128)} %need_ref.1), custom_call_target="tpu_custom_call" | custom-call | flops 8589934592 | bytes 67108864 | tf_op jit(solution)/shard_map/gather_sources/pallas_call | solution.py:182
  51.4 0.0 copy-done
  51.4 0.0 copy-done.1
  51.4 0.0 copy-done.8
  51.4 0.0 copy-done.9
  51.5 0.0 copy-start.2
  51.5 0.0 copy-start.3
  51.5 0.0 copy-start.4
  51.5 0.0 copy-start.5
  51.5 0.0 copy-start.6
  51.5 0.0 copy-start.7
  51.5 0.0 copy-start.10
  51.5 4.9 %spread_rows.1 = bf16[16,128,128]{2,1,0:T(8,128)(2,1)S(1)} custom-call(s32[1,112]{1,0:T(1,128)S(1)} %copy-done.8, s32[1,112]{1,0:T(1,128)S(1)} %copy-done.9, s32[1,1]{1,0:T(1,128)S(6)} %copy.15.count_ref, bf16[9,8,4,2,16,128]{5,4,3,2,1,0:T(8,128)(2,1)S(1)} %gather_sources.1.src_ref, bf16[16,128,128]{2,1,0:T(8,128)(2,1)S(1)} %bitcast.10, ...), custom_call_target="tpu_custom_call" | custom-call | tf_op jit(solution)/shard_map/spread_rows/pallas_call | solution.py:254
  56.5 0.0 copy-done.2
  56.5 0.0 copy-done.3
  56.5 0.0 copy-done.4
  56.5 0.0 copy-done.5
  56.5 0.0 copy-done.6
  56.5 0.0 copy-done.7
  56.5 0.0 copy-done.10
  56.5 17.1 %merge_rows.1 = bf16[4,512,128]{2,1,0:T(8,128)(2,1)S(1)} custom-call(bf16[4,512,128]{2,1,0:T(8,128)(2,1)S(1)} %bitcast.8, bf16[128,128]{1,0:T(8,128)(2,1)S(1)} %copy-done.4, bf16[128,128]{1,0:T(8,128)(2,1)S(1)} %copy-done.5, bf16[128,128]{1,0:T(8,128)(2,1)S(1)} %copy-done.6, bf16[128,128]{1,0:T(8,128)(2,1)S(1)} %copy-done.7, f32[1,128]{1,0:T(1,128)S(1)} %bitcast.11, ...), custom_call_target="tpu_custom_call" | custom-call | tf_op jit(solution)/shard_map/merge_rows/pallas_call | solution.py:383
  73.7 0.8 %copy.16 = bf16[1,2048,128]{2,1,0:T(8,128)(2,1)} copy(bf16[1,2048,128]{2,1,0:T(8,128)(2,1)S(1)} %bitcast.7) | data formatting | bytes 1048576
Async XLA Ops:
  0.7 50.8 %copy-start = (bf16[1,112,128,128]{3,2,1,0:T(8,128)(2,1)S(1)}, bf16[1,112,128,128]{3,2,1,0:T(8,128)(2,1)}, u32[]{:S(2)}) copy-start(bf16[1,112,128,128]{3,2,1,0:T(8,128)(2,1)} %param.14) | copy-start | bytes 11010052
  0.7 50.8 %copy-start.1 = (bf16[2048,128]{1,0:T(8,128)(2,1)S(1)}, bf16[2048,128]{1,0:T(8,128)(2,1)}, u32[]{:S(2)}) copy-start(bf16[2048,128]{1,0:T(8,128)(2,1)} %param.13) | copy-start | bytes 1572868
  0.7 50.8 %copy-start.8 = (s32[1,112]{1,0:T(1,128)S(1)}, s32[1,112]{1,0:T(1,128)}, u32[]{:S(2)}) copy-start(s32[1,112]{1,0:T(1,128)} %rows_ref.1) | copy-start | bytes 1348
  0.7 50.8 %copy-start.9 = (s32[1,112]{1,0:T(1,128)S(1)}, s32[1,112]{1,0:T(1,128)}, u32[]{:S(2)}) copy-start(s32[1,112]{1,0:T(1,128)} %cols_ref.1) | copy-start | bytes 1348
  51.5 5.0 %copy-start.2 = (bf16[128,512]{1,0:T(8,128)(2,1)S(1)}, bf16[128,512]{1,0:T(8,128)(2,1)}, u32[]{:S(2)}) copy-start(bf16[128,512]{1,0:T(8,128)(2,1)} %up_ref.1) | copy-start | bytes 393220
  51.5 5.0 %copy-start.3 = (bf16[512,128]{1,0:T(8,128)(2,1)S(1)}, bf16[512,128]{1,0:T(8,128)(2,1)}, u32[]{:S(2)}) copy-start(bf16[512,128]{1,0:T(8,128)(2,1)} %down_ref.1) | copy-start | bytes 393220
  51.5 5.0 %copy-start.4 = (bf16[128,128]{1,0:T(8,128)(2,1)S(1)}, bf16[128,128]{1,0:T(8,128)(2,1)}, u32[]{:S(2)}) copy-start(bf16[128,128]{1,0:T(8,128)(2,1)} %wq_ref.1) | copy-start | bytes 98308
  51.5 5.0 %copy-start.5 = (bf16[128,128]{1,0:T(8,128)(2,1)S(1)}, bf16[128,128]{1,0:T(8,128)(2,1)}, u32[]{:S(2)}) copy-start(bf16[128,128]{1,0:T(8,128)(2,1)} %wk_ref.1) | copy-start | bytes 98308
  51.5 5.0 %copy-start.6 = (bf16[128,128]{1,0:T(8,128)(2,1)S(1)}, bf16[128,128]{1,0:T(8,128)(2,1)}, u32[]{:S(2)}) copy-start(bf16[128,128]{1,0:T(8,128)(2,1)} %wv_ref.1) | copy-start | bytes 98308
  51.5 5.0 %copy-start.7 = (bf16[128,128]{1,0:T(8,128)(2,1)S(1)}, bf16[128,128]{1,0:T(8,128)(2,1)}, u32[]{:S(2)}) copy-start(bf16[128,128]{1,0:T(8,128)(2,1)} %wo_ref.1) | copy-start | bytes 98308
  51.5 5.0 %copy-start.10 = (f32[128]{0:T(128)S(1)}, f32[128]{0:T(128)}, u32[]{:S(2)}) copy-start(f32[128]{0:T(128)} %param.23) | copy-start | bytes 1540

commit v4 on v3

--- a/solution.py
+++ b/solution.py
@@ -219,7 +219,7 @@
     )
 
 
-GROUP = 4
+GROUP = 16
 TILES = 112
 
 
@@ -268,6 +268,31 @@
 ROWS = 512 // CHUNKS
 
 
+def attend(flat, wide):
+    across = lax.dot_general(
+        wide, flat, (((1,), (1,)), ((), ())), preferred_element_type=jnp.float32
+    )
+    query = across[0:128] * (math.log2(math.e) / math.sqrt(HEAD))
+
+    def heads(rows, b):
+        return rows[:, b * ROWS : (b + 1) * ROWS].reshape(4, HEAD, ROWS)
+
+    key = [heads(across[128:256], b) for b in range(4)]
+    value = [heads(across[256:384], b) for b in range(4)]
+    mixed = []
+    for q in range(4):
+        mine = heads(query, q)
+        scores = [jnp.sum(mine * one, axis=1, keepdims=True) for one in key]
+        top = jnp.maximum(jnp.maximum(scores[0], scores[1]), jnp.maximum(scores[2], scores[3]))
+        weights = [jnp.exp2(one - top) for one in scores]
+        share = 1.0 / ((weights[0] + weights[1]) + (weights[2] + weights[3]))
+        blend = (weights[0] * share) * value[0]
+        for b in range(1, 4):
+            blend = blend + (weights[b] * share) * value[b]
+        mixed.append(blend.reshape(128, ROWS).T.astype(jnp.bfloat16))
+    return jnp.concatenate(mixed, axis=0)
+
+
 def merge_kernel(
     spread_ref,
     wq_ref,
@@ -280,6 +305,7 @@
     out_ref,
     got,
     done,
+    wide,
     own_sem,
     in_send,
     in_recv,
@@ -299,7 +325,7 @@
     @pl.loop(0, CHUNKS)
     def _(c):
         span = pl.ds(pl.multiple_of(c * ROWS, ROWS), ROWS)
-        for i in range(1, 4):
+        for i in (2, 1, 3):
             there = lax.rem(y + i, 4)
             pltpu.make_async_remote_copy(
                 src_ref=spread_ref.at[there, span],
@@ -310,8 +336,8 @@
                 device_id_type=MESH,
             ).start()
 
-    lane = lax.broadcasted_iota(jnp.int32, (128, 128), 0) // HEAD
-    same = (lane == lax.broadcasted_iota(jnp.int32, (128, 128), 1) // HEAD).astype(jnp.bfloat16)
+    for i, ref in enumerate((wq_ref, wk_ref, wv_ref)):
+        wide[i * 128 : (i + 1) * 128] = ref[...].astype(jnp.float32).T.astype(jnp.bfloat16)
     own.wait()
 
     @pl.loop(0, CHUNKS)
@@ -320,32 +346,7 @@
         arrived = got.at[pl.ds(0, 3), span]
         pltpu.make_async_copy(arrived, arrived, in_recv.at[c]).wait()
         flat = got[:, span, :].reshape(4 * ROWS, 128)
-        query = jnp.dot(flat, wq_ref[...], preferred_element_type=jnp.float32)
-        query = query * (math.log2(math.e) / math.sqrt(HEAD))
-        key = jnp.dot(flat, wk_ref[...], preferred_element_type=jnp.float32)
-        value = jnp.dot(flat, wv_ref[...], preferred_element_type=jnp.float32)
-        mixed = []
-        for q in range(4):
-            mine = query[q * ROWS : (q + 1) * ROWS]
-            scores = []
-            for b in range(4):
-                part = mine * key[b * ROWS : (b + 1) * ROWS]
-                high = part.astype(jnp.bfloat16)
-                low = (part - high.astype(jnp.float32)).astype(jnp.bfloat16)
-                scores.append(
-                    jnp.dot(high, same, preferred_element_type=jnp.float32)
-                    + jnp.dot(low, same, preferred_element_type=jnp.float32)
-                )
-            top = jnp.maximum(
-                jnp.maximum(scores[0], scores[1]), jnp.maximum(scores[2], scores[3])
-            )
-            weights = [jnp.exp2(s - top) for s in scores]
-            total = (weights[0] + weights[1]) + (weights[2] + weights[3])
-            blend = weights[0] * value[:ROWS]
-            for b in range(1, 4):
-                blend = blend + weights[b] * value[b * ROWS : (b + 1) * ROWS]
-            mixed.append((blend / total).astype(jnp.bfloat16))
-        mixture = jnp.concatenate(mixed, axis=0)
+        mixture = attend(flat, wide[...])
         residual = flat.astype(jnp.float32) + jnp.dot(
             mixture, wo_ref[...], preferred_element_type=jnp.float32
         )
@@ -356,7 +357,7 @@
         ).astype(jnp.bfloat16)
         result = residual + jnp.dot(hidden, down_ref[...], preferred_element_type=jnp.float32)
         done[:, span, :] = result.astype(jnp.bfloat16).reshape(4, ROWS, 128)
-        for i in range(1, 4):
+        for i in (2, 1, 3):
             there = lax.rem(y + i, 4)
             pltpu.make_async_remote_copy(
                 src_ref=done.at[there, span],
@@ -388,6 +389,7 @@
         scratch_shapes=[
             pltpu.VMEM(quarters, jnp.bfloat16),
             pltpu.VMEM(quarters, jnp.bfloat16),
+            pltpu.VMEM((384, 128), jnp.bfloat16),
             dma,
             dma,
             dma((CHUNKS,)),

time: 74 us -> 71.1 us (0.961); the launches traced: 74.5 us -> 70.8 us
  Pallas kernels: 72.8 us -> 69.1 us
    pallas_call x1, Pallas kernels: 4.91 us -> 1.82 us  [spread_rows(): pl.pallas_call(spread_kernel, out_shape=jax.ShapeDtypeStruct((16, 128, 12...]
where the time goes in v4:
time: 71.1 us; the launch traced here: 70.8 us
  Pallas kernels  69.1 us (97%)
  local copies, waits for them, and re-layouts  0.86 us (1%)
  between operations  0.85 us (1%)
    pallas_call x1, Pallas kernels, gather_sources(): pl.pallas_call(gather_kernel, out_shape=jax.ShapeDtypeStruct((9, 8, 4, 2,...  50.7 us
    pallas_call x1, Pallas kernels, merge_rows(): pl.pallas_call(merge_kernel, out_shape=jax.ShapeDtypeStruct(quarters, jnp...  16.6 us
    pallas_call x1, Pallas kernels, spread_rows(): pl.pallas_call(spread_kernel, out_shape=jax.ShapeDtypeStruct((16, 128, 12...  1.82 us

profile of v4, /device:TPU:1, one launch (start us, length us, event | category | flops | bytes accessed | tf_op | source)
XLA Modules:
  0.0 70.8 jit_solution(3822894730787663221)
XLA Ops:
  0.7 0.0 copy-start
  0.7 0.0 copy-start.1
  0.7 0.0 copy-start.8
  0.7 0.0 copy-start.9
  0.7 50.7 %gather_sources.1.src_ref = bf16[9,8,4,2,16,128]{5,4,3,2,1,0:T(8,128)(2,1)S(1)} custom-call(bf16[16,8,16,128]{3,2,1,0:T(8,128)(2,1)} %bitcast.9, s32[1,64]{1,0:T(1,128)} %need_ref.1), custom_call_target="tpu_custom_call" | custom-call | flops 8589934592 | bytes 67108864 | tf_op jit(solution)/shard_map/gather_sources/pallas_call | solution.py:182
  51.4 0.0 copy-done
  51.4 0.0 copy-done.1
  51.4 0.0 copy-done.8
  51.4 0.0 copy-done.9
  51.5 0.0 copy-start.2
  51.5 0.0 copy-start.3
  51.5 0.0 copy-start.4
  51.5 0.0 copy-start.5
  51.5 0.0 copy-start.6
  51.5 0.0 copy-start.7
  51.5 0.0 copy-start.10
  51.5 1.8 %spread_rows.1 = bf16[16,128,128]{2,1,0:T(8,128)(2,1)S(1)} custom-call(s32[1,112]{1,0:T(1,128)S(1)} %copy-done.8, s32[1,112]{1,0:T(1,128)S(1)} %copy-done.9, s32[1,1]{1,0:T(1,128)S(6)} %copy.15.count_ref, bf16[9,8,4,2,16,128]{5,4,3,2,1,0:T(8,128)(2,1)S(1)} %gather_sources.1.src_ref, bf16[16,128,128]{2,1,0:T(8,128)(2,1)S(1)} %bitcast.10, ...), custom_call_target="tpu_custom_call" | custom-call | tf_op jit(solution)/shard_map/spread_rows/pallas_call | solution.py:254
  53.4 0.0 copy-done.2
  53.4 0.0 copy-done.3
  53.4 0.0 copy-done.4
  53.4 0.0 copy-done.5
  53.4 0.0 copy-done.6
  53.4 0.0 copy-done.7
  53.4 0.0 copy-done.10
  53.4 16.6 %merge_rows.1 = bf16[4,512,128]{2,1,0:T(8,128)(2,1)S(1)} custom-call(bf16[4,512,128]{2,1,0:T(8,128)(2,1)S(1)} %bitcast.8, bf16[128,128]{1,0:T(8,128)(2,1)S(1)} %copy-done.4, bf16[128,128]{1,0:T(8,128)(2,1)S(1)} %copy-done.5, bf16[128,128]{1,0:T(8,128)(2,1)S(1)} %copy-done.6, bf16[128,128]{1,0:T(8,128)(2,1)S(1)} %copy-done.7, f32[1,128]{1,0:T(1,128)S(1)} %bitcast.11, ...), custom_call_target="tpu_custom_call" | custom-call | tf_op jit(solution)/shard_map/merge_rows/pallas_call | solution.py:384
  70.0 0.8 %copy.16 = bf16[1,2048,128]{2,1,0:T(8,128)(2,1)} copy(bf16[1,2048,128]{2,1,0:T(8,128)(2,1)S(1)} %bitcast.7) | data formatting | bytes 1048576
Async XLA Ops:
  0.7 50.8 %copy-start = (bf16[1,112,128,128]{3,2,1,0:T(8,128)(2,1)S(1)}, bf16[1,112,128,128]{3,2,1,0:T(8,128)(2,1)}, u32[]{:S(2)}) copy-start(bf16[1,112,128,128]{3,2,1,0:T(8,128)(2,1)} %param.14) | copy-start | bytes 11010052
  0.7 50.8 %copy-start.1 = (bf16[2048,128]{1,0:T(8,128)(2,1)S(1)}, bf16[2048,128]{1,0:T(8,128)(2,1)}, u32[]{:S(2)}) copy-start(bf16[2048,128]{1,0:T(8,128)(2,1)} %param.13) | copy-start | bytes 1572868
  0.7 50.8 %copy-start.8 = (s32[1,112]{1,0:T(1,128)S(1)}, s32[1,112]{1,0:T(1,128)}, u32[]{:S(2)}) copy-start(s32[1,112]{1,0:T(1,128)} %rows_ref.1) | copy-start | bytes 1348
  0.7 50.8 %copy-start.9 = (s32[1,112]{1,0:T(1,128)S(1)}, s32[1,112]{1,0:T(1,128)}, u32[]{:S(2)}) copy-start(s32[1,112]{1,0:T(1,128)} %cols_ref.1) | copy-start | bytes 1348
  51.5 1.9 %copy-start.2 = (bf16[128,512]{1,0:T(8,128)(2,1)S(1)}, bf16[128,512]{1,0:T(8,128)(2,1)}, u32[]{:S(2)}) copy-start(bf16[128,512]{1,0:T(8,128)(2,1)} %up_ref.1) | copy-start | bytes 393220
  51.5 1.9 %copy-start.3 = (bf16[512,128]{1,0:T(8,128)(2,1)S(1)}, bf16[512,128]{1,0:T(8,128)(2,1)}, u32[]{:S(2)}) copy-start(bf16[512,128]{1,0:T(8,128)(2,1)} %down_ref.1) | copy-start | bytes 393220
  51.5 1.9 %copy-start.4 = (bf16[128,128]{1,0:T(8,128)(2,1)S(1)}, bf16[128,128]{1,0:T(8,128)(2,1)}, u32[]{:S(2)}) copy-start(bf16[128,128]{1,0:T(8,128)(2,1)} %wq_ref.1) | copy-start | bytes 98308
  51.5 1.9 %copy-start.5 = (bf16[128,128]{1,0:T(8,128)(2,1)S(1)}, bf16[128,128]{1,0:T(8,128)(2,1)}, u32[]{:S(2)}) copy-start(bf16[128,128]{1,0:T(8,128)(2,1)} %wk_ref.1) | copy-start | bytes 98308
  51.5 1.9 %copy-start.6 = (bf16[128,128]{1,0:T(8,128)(2,1)S(1)}, bf16[128,128]{1,0:T(8,128)(2,1)}, u32[]{:S(2)}) copy-start(bf16[128,128]{1,0:T(8,128)(2,1)} %wv_ref.1) | copy-start | bytes 98308
  51.5 1.9 %copy-start.7 = (bf16[128,128]{1,0:T(8,128)(2,1)S(1)}, bf16[128,128]{1,0:T(8,128)(2,1)}, u32[]{:S(2)}) copy-start(bf16[128,128]{1,0:T(8,128)(2,1)} %wo_ref.1) | copy-start | bytes 98308
  51.5 1.9 %copy-start.10 = (f32[128]{0:T(128)S(1)}, f32[128]{0:T(128)}, u32[]{:S(2)}) copy-start(f32[128]{0:T(128)} %param.23) | copy-start | bytes 1540

commit v5 on v4

--- a/solution.py
+++ b/solution.py
@@ -13,7 +13,7 @@
 STEPS = 8
 FAR_FIRST = sorted(
     ((i, j) for i in range(4) for j in range(8) if i or j),
-    key=lambda at: -(min(at[0], 4 - at[0]) * 2 + min(at[1], 8 - at[1])),
+    key=lambda at: (-(min(at[0], 4 - at[0]) * 2 + min(at[1], 8 - at[1])) , (at[0] + at[1]) % 2),
 )
 
 
@@ -29,9 +29,9 @@
 
 def gather_kernel(emb_ref, need_ref, out_ref, *scratch):
     chunks = scratch[:9]
-    picked, mid, need_x, need_v, need_s = scratch[9:14]
-    own_sem, pair_send, pair_recv, ring_send, ring_recv = scratch[14:19]
-    ask_send, ask_recv, smem_sem, x_send, x_recv, y_send, y_recv = scratch[19:]
+    picked, need_x, need_v, need_s = scratch[9:13]
+    own_sem, pair_send, pair_recv, ring_send, ring_recv = scratch[13:18]
+    ask_send, ask_recv, smem_sem, need_sem, y_send, y_recv = scratch[18:]
     x, y, z, k = place()
     part = y * 2 + k
     above = device(x, y, lax.rem(z + 1, 16), k)
@@ -61,7 +61,8 @@
         emb_ref.at[:, part], chunks[0].at[pl.ds(k * 16, 16)], own_sem
     )
     own.start()
-    pltpu.make_async_copy(need_ref, need_x.at[x], ask_recv.at[0]).start()
+    mine = pltpu.make_async_copy(need_ref, need_x.at[x], need_sem)
+    mine.start()
 
     barrier = pltpu.get_barrier_semaphore()
     for peer in (above, below, *row_peers[1:], *part_peers[1:]):
@@ -126,8 +127,9 @@
                 device(rows[i], parts[j] // 2, z, lax.rem(parts[j], 2)),
             )
 
-    for peer in row_peers[1:]:
-        send(need_ref, need_x.at[x], ask_send.at[0], ask_recv.at[0], peer)
+    mine.wait()
+    for i in (2, 1, 3):
+        send(need_x.at[x], need_x.at[x], ask_send.at[0], ask_recv.at[0], row_peers[i])
     pair = send(
         emb_ref.at[:, y * 2 + 1 - k],
         chunks[0].at[pl.ds(k * 16, 16)],
@@ -138,20 +140,17 @@
     own.wait()
     forward(0, 0)
     forward(0, 1)
-    wait_bytes(need_x, ask_recv.at[0])
-    for peer in part_peers[1:]:
-        send(need_x, need_v.at[part], ask_send.at[1], ask_recv.at[1], peer)
-    pltpu.make_async_copy(need_x, need_v.at[part], ask_recv.at[1]).start()
+    wait_bytes(need_x.at[pl.ds(0, 3)], ask_recv.at[0])
+    for i in (4, 5, 3, 2, 6, 7, 1):
+        send(need_x, need_s.at[part], ask_send.at[1], ask_recv.at[1], part_peers[i])
+    pltpu.make_async_copy(need_x, need_s.at[part], ask_recv.at[1]).start()
     pair.wait_recv()
     forward(0, 2)
     forward(0, 3)
     forward(1, 0)
     forward(1, 1)
-    wait_bytes(need_v, ask_recv.at[1])
-    table = pltpu.make_async_copy(need_v, need_s, smem_sem)
-    table.start()
+    wait_bytes(need_s, ask_recv.at[1])
     forward(1, 2)
-    table.wait()
     forward(1, 3)
     pick(0)
     deliver(0)
@@ -189,7 +188,6 @@
             *([two] * 7),
             one,
             picks,
-            pltpu.VMEM((8, 128), jnp.float32),
             pltpu.VMEM((4, 1, 64), jnp.int32),
             pltpu.VMEM((8, 4, 1, 64), jnp.int32),
             pltpu.SMEM((8, 4, 1, 64), jnp.int32),
@@ -201,8 +199,7 @@
             dma((2,)),
             dma((2,)),
             dma,
-            dma((3,)),
-            dma((9,)),
+            dma,
             dma((3,)),
             dma((3,)),
         ],

time: 71.1 us -> 71.4 us (level)
  no operation moved by 1% of the time
where the time goes in v5:
time: 71.4 us; the launch traced here: 71.2 us
  Pallas kernels  69.5 us (97%)
  local copies, waits for them, and re-layouts  0.86 us (1%)
  between operations  0.85 us (1%)
    pallas_call x1, Pallas kernels, gather_sources(): pl.pallas_call(gather_kernel, out_shape=jax.ShapeDtypeStruct((9, 8, 4, 2,...  50.9 us
    pallas_call x1, Pallas kernels, merge_rows(): pl.pallas_call(merge_kernel, out_shape=jax.ShapeDtypeStruct(quarters, jnp...  16.8 us
    pallas_call x1, Pallas kernels, spread_rows(): pl.pallas_call(spread_kernel, out_shape=jax.ShapeDtypeStruct((16, 128, 12...  1.82 us

profile of v5, /device:TPU:1, one launch (start us, length us, event | category | flops | bytes accessed | tf_op | source)
XLA Modules:
  0.0 71.2 jit_solution(12827502902279103878)
XLA Ops:
  0.7 0.0 copy-start
  0.7 0.0 copy-start.1
  0.7 0.0 copy-start.8
  0.7 0.0 copy-start.9
  0.7 50.9 %gather_sources.1.src_ref = bf16[9,8,4,2,16,128]{5,4,3,2,1,0:T(8,128)(2,1)S(1)} custom-call(bf16[16,8,16,128]{3,2,1,0:T(8,128)(2,1)} %bitcast.9, s32[1,64]{1,0:T(1,128)} %need_ref.1), custom_call_target="tpu_custom_call" | custom-call | flops 8589934592 | bytes 67108864 | tf_op jit(solution)/shard_map/gather_sources/pallas_call | solution.py:181
  51.6 0.0 copy-done
  51.6 0.0 copy-done.1
  51.6 0.0 copy-done.8
  51.6 0.0 copy-done.9
  51.6 0.0 copy-start.2
  51.6 0.0 copy-start.3
  51.6 0.0 copy-start.4
  51.7 0.0 copy-start.5
  51.7 0.0 copy-start.6
  51.7 0.0 copy-start.7
  51.7 0.0 copy-start.10
  51.7 1.8 %spread_rows.1 = bf16[16,128,128]{2,1,0:T(8,128)(2,1)S(1)} custom-call(s32[1,112]{1,0:T(1,128)S(1)} %copy-done.8, s32[1,112]{1,0:T(1,128)S(1)} %copy-done.9, s32[1,1]{1,0:T(1,128)S(6)} %copy.15.count_ref, bf16[9,8,4,2,16,128]{5,4,3,2,1,0:T(8,128)(2,1)S(1)} %gather_sources.1.src_ref, bf16[16,128,128]{2,1,0:T(8,128)(2,1)S(1)} %bitcast.10, ...), custom_call_target="tpu_custom_call" | custom-call | tf_op jit(solution)/shard_map/spread_rows/pallas_call | solution.py:251
  53.5 0.0 copy-done.2
  53.5 0.0 copy-done.3
  53.6 0.0 copy-done.4
  53.6 0.0 copy-done.5
  53.6 0.0 copy-done.6
  53.6 0.0 copy-done.7
  53.6 0.0 copy-done.10
  53.6 16.8 %merge_rows.1 = bf16[4,512,128]{2,1,0:T(8,128)(2,1)S(1)} custom-call(bf16[4,512,128]{2,1,0:T(8,128)(2,1)S(1)} %bitcast.8, bf16[128,128]{1,0:T(8,128)(2,1)S(1)} %copy-done.4, bf16[128,128]{1,0:T(8,128)(2,1)S(1)} %copy-done.5, bf16[128,128]{1,0:T(8,128)(2,1)S(1)} %copy-done.6, bf16[128,128]{1,0:T(8,128)(2,1)S(1)} %copy-done.7, f32[1,128]{1,0:T(1,128)S(1)} %bitcast.11, ...), custom_call_target="tpu_custom_call" | custom-call | tf_op jit(solution)/shard_map/merge_rows/pallas_call | solution.py:381
  70.5 0.8 %copy.16 = bf16[1,2048,128]{2,1,0:T(8,128)(2,1)} copy(bf16[1,2048,128]{2,1,0:T(8,128)(2,1)S(1)} %bitcast.7) | data formatting | bytes 1048576
Async XLA Ops:
  0.7 50.9 %copy-start = (bf16[1,112,128,128]{3,2,1,0:T(8,128)(2,1)S(1)}, bf16[1,112,128,128]{3,2,1,0:T(8,128)(2,1)}, u32[]{:S(2)}) copy-start(bf16[1,112,128,128]{3,2,1,0:T(8,128)(2,1)} %param.14) | copy-start | bytes 11010052
  0.7 50.9 %copy-start.1 = (bf16[2048,128]{1,0:T(8,128)(2,1)S(1)}, bf16[2048,128]{1,0:T(8,128)(2,1)}, u32[]{:S(2)}) copy-start(bf16[2048,128]{1,0:T(8,128)(2,1)} %param.13) | copy-start | bytes 1572868
  0.7 50.9 %copy-start.8 = (s32[1,112]{1,0:T(1,128)S(1)}, s32[1,112]{1,0:T(1,128)}, u32[]{:S(2)}) copy-start(s32[1,112]{1,0:T(1,128)} %rows_ref.1) | copy-start | bytes 1348
  0.7 50.9 %copy-start.9 = (s32[1,112]{1,0:T(1,128)S(1)}, s32[1,112]{1,0:T(1,128)}, u32[]{:S(2)}) copy-start(s32[1,112]{1,0:T(1,128)} %cols_ref.1) | copy-start | bytes 1348
  51.6 1.9 %copy-start.2 = (bf16[128,512]{1,0:T(8,128)(2,1)S(1)}, bf16[128,512]{1,0:T(8,128)(2,1)}, u32[]{:S(2)}) copy-start(bf16[128,512]{1,0:T(8,128)(2,1)} %up_ref.1) | copy-start | bytes 393220
  51.6 1.9 %copy-start.3 = (bf16[512,128]{1,0:T(8,128)(2,1)S(1)}, bf16[512,128]{1,0:T(8,128)(2,1)}, u32[]{:S(2)}) copy-start(bf16[512,128]{1,0:T(8,128)(2,1)} %down_ref.1) | copy-start | bytes 393220
  51.6 1.9 %copy-start.4 = (bf16[128,128]{1,0:T(8,128)(2,1)S(1)}, bf16[128,128]{1,0:T(8,128)(2,1)}, u32[]{:S(2)}) copy-start(bf16[128,128]{1,0:T(8,128)(2,1)} %wq_ref.1) | copy-start | bytes 98308
  51.7 1.9 %copy-start.5 = (bf16[128,128]{1,0:T(8,128)(2,1)S(1)}, bf16[128,128]{1,0:T(8,128)(2,1)}, u32[]{:S(2)}) copy-start(bf16[128,128]{1,0:T(8,128)(2,1)} %wk_ref.1) | copy-start | bytes 98308
  51.7 1.9 %copy-start.6 = (bf16[128,128]{1,0:T(8,128)(2,1)S(1)}, bf16[128,128]{1,0:T(8,128)(2,1)}, u32[]{:S(2)}) copy-start(bf16[128,128]{1,0:T(8,128)(2,1)} %wv_ref.1) | copy-start | bytes 98308
  51.7 1.9 %copy-start.7 = (bf16[128,128]{1,0:T(8,128)(2,1)S(1)}, bf16[128,128]{1,0:T(8,128)(2,1)}, u32[]{:S(2)}) copy-start(bf16[128,128]{1,0:T(8,128)(2,1)} %wo_ref.1) | copy-start | bytes 98308
  51.7 1.9 %copy-start.10 = (f32[128]{0:T(128)S(1)}, f32[128]{0:T(128)}, u32[]{:S(2)}) copy-start(f32[128]{0:T(128)} %param.23) | copy-start | bytes 1540
